TPU v7x, 32 devices: a whole 2x2x4 slice. The times are simulated.
32 devices in a mesh: section: 2 (over x), dp: 4 (over y, core), expert: 4 (over z).
Axes of the slice: x: 2, y: 2, z: 4, core: 2. Of those that a mesh axis runs over, the one named last changes fastest.
Arguments:
- tokens: bfloat16 [2, 2048, 2560], P('section', ('dp', 'expert')), may hold values from -6 to 6
- cotangent: bfloat16 [2, 2048, 2560], P('section', ('dp', 'expert')), may hold values from -3 to 3
- routes: int32 [2, 2048, 6], P('section', ('dp', 'expert')), may hold values from 0 to 159, as said below
- gates: float32 [2, 2048, 6], P('section', ('dp', 'expert')), may hold values from 0.2 to 1
- gate_up: bfloat16 [2, 4, 2, 1024, 2560], P('section', 'expert', None, 'dp'), may hold values from -0.125 to 0.125
- down: bfloat16 [2, 4, 1024, 2560], P('section', 'expert', 'dp'), may hold values from -0.1875 to 0.1875
Outputs:
- handed_on: bfloat16 [2, 2048, 2560], P('section', ('dp', 'expert'))
- handed_back: bfloat16 [2, 2048, 2560], P('section', ('dp', 'expert'))
- grad_gate_up: bfloat16 [2, 4, 2, 1024, 2560], P('section', 'expert', None, 'dp')
- grad_down: bfloat16 [2, 4, 1024, 2560], P('section', 'expert', 'dp')
Inputs may be any that keep to these rules, and one draw needn't show every extreme that they name: `routes`: A token's 6 ids are distinct and at most one of them is below 4. In each device's block of 128 tokens no id below 4 is named by more than 32 tokens.
All inputs are finite; a program needn't handle non-finite values.
Results may differ from a plain program's by a relative error of at most 0.0065.
Values may be sent and summed in bfloat16 or wider, within the bound.
No kernel may reach another device: no remote copies, remote signals or barrier semaphores. Data moves between devices by JAX's collectives and lax.ppermute only.
A program may use at most 64 MiB of HBM per device.

v0:
```python
import functools

import jax
import jax.numpy as jnp
from jax import lax
from jax.experimental import pallas as pl
from jax.experimental.pallas import tpu as pltpu
from jax.sharding import PartitionSpec as P


AXES = ("section", "dp", "expert")
LAST = (((1,), (1,)), ((), ()))
FIRST = (((0,), (0,)), ((), ()))
PLAIN = (((1,), (0,)), ((), ()))
IN_VMEM = pl.BlockSpec(memory_space=pltpu.VMEM)
IN_HBM = pl.BlockSpec(memory_space=pltpu.HBM)
IN_SMEM = pl.BlockSpec(memory_space=pltpu.SMEM)


def moved(value, target):
    sizes = [lax.axis_size(axis) for axis in AXES]
    pairs = []
    for s in range(sizes[0]):
        for d in range(sizes[1]):
            for e in range(sizes[2]):
                to = target(s, d, e)
                if to is not None:
                    source = (s * sizes[1] + d) * sizes[2] + e
                    pairs.append((source, (to[0] * sizes[1] + to[1]) * sizes[2] + to[2]))
    return lax.ppermute(value, AXES, pairs)


def in_hbm(value):
    return pltpu.with_memory_space_constraint(value, pltpu.HBM)


def dot(a, b, dims=PLAIN):
    return lax.dot_general(a, b, dims, preferred_element_type=jnp.float32)


def call(body, outs, operands, mib, scratch=(), smem=1):
    return pl.pallas_call(
        body,
        out_shape=outs,
        in_specs=[IN_SMEM] * smem + [IN_VMEM] * (len(operands) - smem),
        out_specs=[IN_VMEM] * len(outs),
        scratch_shapes=scratch,
        compiler_params=pltpu.CompilerParams(vmem_limit_bytes=mib << 20),
    )(*operands)


def column_of(row):
    n = row.shape[1]
    diagonal = lax.broadcasted_iota(jnp.int32, (n, n), 0) == lax.broadcasted_iota(jnp.int32, (n, n), 1)
    return jnp.sum(jnp.where(diagonal, row, 0.0), 1, keepdims=True)


def pack_body(window, units, lanes, where_ref, routes, gates, tokens, cotangent, *refs):
    section, column = where_ref[0], where_ref[1]
    packed, info, refs = refs[: len(units)], refs[len(units)], refs[len(units) + 1 :]
    tokens_here, cotangent_here, routes_here, gates_here, sems, small_sems = refs
    rows_here, width = tokens.shape
    capacity = rows_here // window
    blocks = 4 if width % 512 == 0 else 1
    step = width // blocks
    small = [
        pltpu.make_async_copy(far, near, small_sems.at[which])
        for which, (far, near) in enumerate(((routes, routes_here), (gates, gates_here)))
    ]
    for copy in small:
        copy.start()
    copies = []
    for which, (far, near) in enumerate(((tokens, tokens_here), (cotangent, cotangent_here))):
        for b in range(blocks):
            at = pl.ds(b * step, step)
            copies.append(pltpu.make_async_copy(far.at[:, at], near.at[:, at], sems.at[which, b]))
            copies[-1].start()
    for copy in small:
        copy.wait()
    expert_of = jnp.full((1, rows_here), -1, jnp.int32)
    weight = jnp.zeros((1, rows_here), jnp.float32)
    for i in range(routes.shape[0]):
        in_window = routes_here[i] < window
        expert_of = jnp.where(in_window, routes_here[i], expert_of)
        weight = jnp.where(in_window, gates_here[i], weight)
    present = expert_of >= 0
    distance = expert_of - column
    distance = jnp.where(distance < 0, distance + window, distance)
    code = jnp.where(present, distance, -1).astype(jnp.float32)
    square = (rows_here, rows_here)
    down_index = lax.broadcasted_iota(jnp.int32, square, 0)
    along_index = lax.broadcasted_iota(jnp.int32, square, 1)
    earlier = (column_of(code) == code) & (down_index < along_index)
    slot = jnp.sum(jnp.where(earlier, 1.0, 0.0), 0, keepdims=True)
    place = jnp.where(present, code * capacity + slot, -1.0)
    select = jnp.where(down_index.astype(jnp.float32) == place, 1.0, 0.0).astype(jnp.bfloat16)
    for i, (kind, _) in enumerate(lanes):
        ones = jnp.ones_like(weight)
        scale = {"up": weight, "down": ones, "swap": jnp.where(section == 0, weight, ones)}[kind]
        info[i, 0:1] = place
        info[i, 1:2] = scale
    scale_column = column_of(weight)
    for which in range(2):
        for b in range(blocks):
            at = slice(b * step, (b + 1) * step)
            copies[which * blocks + b].wait()
            if which:
                block = (cotangent_here[:, at].astype(jnp.float32) * scale_column).astype(jnp.bfloat16)
            else:
                block = tokens_here[:, at]
            slots = dot(select, block).astype(jnp.bfloat16)
            for out, (k, low, high) in zip(packed, units):
                out[which, :, at] = slots[k * capacity + low : k * capacity + high]


def fetch_body(blocks, gate_up, down, gate_up_out, down_out, sems):
    copies = []
    for which, (far, near) in enumerate(((gate_up.at[0], gate_up_out.at[0]), (gate_up.at[1], gate_up_out.at[1]), (down, down_out))):
        step = far.shape[0] // blocks
        for b in range(blocks):
            at = pl.ds(b * step, step)
            copies.append(pltpu.make_async_copy(far.at[at], near.at[at], sems.at[which, b]))
            copies[-1].start()
    for copy in copies:
        copy.wait()


def chunk_body(lanes, groups, merges, where_ref, *refs):
    section = where_ref[0]
    count = groups * sum(len(merge) for merge in merges)
    pieces, refs = refs[:count], refs[count:]
    (gate_up_here, down_here, gate_up_pair, down_pair), refs = refs[:4], refs[4:]
    outs, (kept, bundle) = refs[:-2], refs[-2:]
    units, width = down_here.shape
    bounds = [0]
    for piece in pieces:
        bounds.append(bounds[-1] + piece.shape[1])
        at = slice(bounds[-2], bounds[-1])
        bundle[at, :width] = piece[0]
        bundle[at, width : 2 * width] = piece[1]
    rows, grads = bundle[:, :width], bundle[:, width : 2 * width]
    sent = bundle.at[:, 2 * width :]
    for gate_up, down, hidden_out in ((gate_up_here, down_here, kept), (gate_up_pair, down_pair, sent)):
        pre_gate = dot(rows, gate_up[0], LAST)
        pre_up = dot(rows, gate_up[1], LAST)
        hidden_grad = dot(grads, down[...], LAST)
        sigmoid = jax.nn.sigmoid(pre_gate)
        activated = pre_gate * sigmoid
        slope = sigmoid * (1.0 + pre_gate * (1.0 - sigmoid))
        hidden_out[:, :units] = (activated * pre_up).astype(jnp.bfloat16)
        hidden_out[:, units : 2 * units] = (hidden_grad * pre_up * slope).astype(jnp.bfloat16)
        hidden_out[:, 2 * units :] = (hidden_grad * activated).astype(jnp.bfloat16)

    def output_rows():
        return dot(kept[:, :units], down_here[...]) + dot(sent[:, :units], down_pair[...])

    def input_rows():
        total = None
        for gate_up, hidden in ((gate_up_here, kept), (gate_up_pair, sent)):
            for i in range(2):
                term = dot(hidden[:, (i + 1) * units : (i + 2) * units], gate_up[i])
                total = term if total is None else total + term
        return total

    def store(i, total):
        for m, merge in enumerate(merges):
            for j in range(groups):
                out = outs[(i * len(merges) + m) * groups + j]
                at = 0
                for u in merge:
                    low, high = bounds[u * groups + j], bounds[u * groups + j + 1]
                    out[at : at + high - low] = total[low:high].astype(out.dtype)
                    at += high - low

    for i, (kind, _) in enumerate(lanes):
        if kind == "up":
            store(i, output_rows())
        elif kind == "down":
            store(i, input_rows())
        else:

            @pl.when(section == 0)
            def _():
                store(i, output_rows())

            @pl.when(section != 0)
            def _():
                store(i, input_rows())


def weights_body(which, columns, hidden_refs, piece_refs, bundles, out, hidden_all, piece_all):
    units, width = out.shape[1:]
    at = 0
    for ref in hidden_refs:
        hidden_all[at : at + ref.shape[0]] = ref[...]
        at += ref.shape[0]
    at = 0
    for ref in piece_refs:
        piece_all[at : at + ref.shape[1]] = ref[which]
        at += ref.shape[1]
    for ref in bundles:
        piece_all[at : at + ref.shape[0]] = ref[:, which * width : (which + 1) * width]
        hidden_all[at : at + ref.shape[0]] = ref[:, 2 * width :]
        at += ref.shape[0]
    for i, c in enumerate(columns):
        value = dot(hidden_all[:, c * units : (c + 1) * units], piece_all[...], FIRST)
        out[i] = value.astype(out.dtype)


def final_body(mode, returns, where_ref, info, *refs):
    section = where_ref[0]
    sorted_refs = [refs[r] for r in sorted(range(len(returns)), key=lambda r: returns[r])]
    rows = jnp.concatenate([ref[...] for ref in sorted_refs])
    outs = refs[len(returns) :]
    place, scale = info[0:1], info[1:2]
    size = (rows.shape[0], place.shape[1])
    pick = jnp.where(lax.broadcasted_iota(jnp.int32, size, 0).astype(jnp.float32) == place, 1.0, 0.0)
    value = dot(pick.astype(jnp.bfloat16), rows, FIRST) * column_of(scale)
    value = value.astype(jnp.bfloat16)
    zero = jnp.zeros_like(value)
    for out, (lowest, highest) in zip(outs, mode):
        keep = (section >= lowest) & (section <= highest)
        out[...] = jnp.where(keep, value, zero)


def plan(window, capacity):
    if window < 4:
        units = [(k, 0, capacity) for k in range(window)]
        return units, [[[k] for k in range(window)]]
    half = capacity // 2
    units = [(k, 0, capacity) for k in range(2)]
    for k in range(2, window):
        units += [(k, 0, half), (k, half, capacity)]
    pairs = [[[u, u + 1]] for u in range(2, len(units), 2)]
    return units, [[[0]], [[1]]] + pairs


def computed(tokens, cotangent, routes, gates, gate_up, down):
    sections, copies, window = (lax.axis_size(axis) for axis in AXES)
    groups = copies // 2
    rows_here, width = tokens.shape[1:]
    capacity = rows_here // window
    position = jnp.stack([lax.axis_index("section"), lax.axis_index("expert")]).astype(jnp.int32)

    def pair_of(s, d, e):
        return s, d ^ 1, e

    def group_shift(step):
        return lambda s, d, e: (s, (d // 2 + step) % groups * 2 + d % 2, e)

    def column_shift(step):
        return lambda s, d, e: (s, d, (e + step) % window)

    def owner_shift(up, step):
        def target(s, d, e):
            to = (s + up) % sections if sections == 2 else s + up
            return (to, d, (e + step) % window) if 0 <= to < sections else None

        return target

    lanes = (("swap", 1),) if sections == 2 else (("up", 1), ("down", -1))
    bf16 = functools.partial(jax.ShapeDtypeStruct, dtype=jnp.bfloat16)
    f32 = functools.partial(jax.ShapeDtypeStruct, dtype=jnp.float32)

    units, chunks = plan(window, capacity)
    step = width // 4 if width % 512 == 0 else width
    *packed, info = pl.pallas_call(
        functools.partial(pack_body, window, units, lanes),
        out_shape=[bf16((2, high - low, width)) for _, low, high in units] + [f32((len(lanes), 2, rows_here))],
        in_specs=[IN_SMEM] + [IN_HBM] * 4,
        out_specs=[IN_VMEM] * (len(units) + 1),
        scratch_shapes=[pltpu.VMEM((rows_here, width), jnp.bfloat16)] * 2
        + [pltpu.VMEM((routes.shape[2], 1, rows_here), dtype) for dtype in (routes.dtype, gates.dtype)]
        + [pltpu.SemaphoreType.DMA((2, width // step)), pltpu.SemaphoreType.DMA((2,))],
        compiler_params=pltpu.CompilerParams(vmem_limit_bytes=12 << 20),
        name="pack",
    )(
        position,
        in_hbm(jnp.transpose(routes, (2, 0, 1))),
        in_hbm(jnp.transpose(gates, (2, 0, 1))),
        in_hbm(tokens[0]),
        in_hbm(cotangent[0]),
    )
    infos = [moved(info[i], owner_shift(up, 0)) for i, (_, up) in enumerate(lanes)]

    gate_up_here, down_here = gate_up[0, 0], down[0, 0]
    gate_up_pair = moved(gate_up_here, pair_of)
    down_pair = moved(down_here, pair_of)
    hidden_units = down_here.shape[0]
    gate_up_here, down_here = pl.pallas_call(
        functools.partial(fetch_body, 2),
        out_shape=[bf16(gate_up_here.shape), bf16(down_here.shape)],
        in_specs=[IN_HBM] * 2,
        out_specs=[IN_VMEM] * 2,
        scratch_shapes=[pltpu.SemaphoreType.DMA((3, 2))],
        compiler_params=pltpu.CompilerParams(vmem_limit_bytes=12 << 20),
        name="fetch",
    )(in_hbm(gate_up_here), in_hbm(down_here))
    weights = (gate_up_here, down_here, gate_up_pair, down_pair)
    weights = tuple(pltpu.with_memory_space_constraint(w, pltpu.VMEM) for w in weights)

    arrived = [moved(packed[u], column_shift(k)) if k else packed[u] for u, (k, _, _) in enumerate(units)]
    returned = [[] for _ in lanes]
    returns = []
    kept_pieces, kept_hidden, bundles = [], [], []
    for chunk in chunks:
        pieces, part_shapes, merges = [], [], []
        for merge in chunk:
            merges.append([len(pieces) // groups + m for m in range(len(merge))])
            for u in merge:
                pieces += [moved(arrived[u], group_shift(j)) if j else arrived[u] for j in range(groups)]
            size = (sum(units[u][2] - units[u][1] for u in merge), width)
            part_shapes += [f32(size)] + [bf16(size)] * (groups - 1)
            returns.append(units[merge[0]])
        chunk_rows = sum(piece.shape[1] for piece in pieces)
        *parts, kept, bundle = call(
            functools.partial(chunk_body, lanes, groups, merges),
            part_shapes * len(lanes)
            + [bf16((chunk_rows, 3 * hidden_units)), bf16((chunk_rows, 2 * width + 3 * hidden_units))],
            (position, *pieces, *weights),
            16,
        )
        kept_pieces += pieces
        kept_hidden.append(kept)
        bundles.append(moved(bundle, pair_of))
        for i, (_, up) in enumerate(lanes):
            for m, merge in enumerate(chunk):
                at = (i * len(chunk) + m) * groups
                total = parts[at]
                for j in range(1, groups):
                    back = moved(parts[at + j], group_shift(-j))
                    total = total + back.astype(jnp.float32)
                returned[i].append(moved(total.astype(jnp.bfloat16), owner_shift(up, -units[merge[0]][0])))

    def weights_call(which, columns):
        operands = (*kept_hidden, *kept_pieces, *bundles)
        n, m = len(kept_hidden), len(kept_hidden) + len(kept_pieces)

        def body(*refs):
            at = len(operands)
            weights_body(which, columns, refs[:n], refs[n:m], refs[m:at], *refs[at:])

        contracted = 2 * sum(piece.shape[1] for piece in kept_pieces)
        return call(
            body,
            [bf16((len(columns), hidden_units, width))],
            operands,
            16,
            [
                pltpu.VMEM((contracted, 3 * hidden_units), jnp.bfloat16),
                pltpu.VMEM((contracted, width), jnp.bfloat16),
            ],
            smem=0,
        )[0]

    grad_down = weights_call(1, (0,))
    grad_gate_up = weights_call(0, (1, 2))

    modes = {
        "swap": ((1, 1), (0, 0)),
        "up": ((1, sections - 1),),
        "down": ((0, sections - 2),),
    }
    results = []
    for i, (kind, _) in enumerate(lanes):
        results += call(
            functools.partial(final_body, modes[kind], returns),
            [bf16((rows_here, width))] * len(modes[kind]),
            (position, infos[i], *returned[i]),
            12,
        )
    return (results[0][None], results[1][None], grad_gate_up[None, None], grad_down[None])


def solution(mesh):
    tokens_spec = P("section", ("dp", "expert"), None)
    gate_up_spec = P("section", "expert", None, "dp", None)
    down_spec = P("section", "expert", "dp", None)
    return jax.shard_map(
        computed,
        mesh=mesh,
        in_specs=(tokens_spec,) * 4 + (gate_up_spec, down_spec),
        out_specs=(tokens_spec, tokens_spec, gate_up_spec, down_spec),
        check_vma=False,
    )
```

profile of v0, /device:TPU:0, one launch (start us, length us, event | category | flops | bytes accessed | tf_op | source)
XLA Modules:
  0.0 110.1 jit_solution(4722333966815668667)
XLA Ops:
  1.3 3.5 %pack.1 = (bf16[2,32,2560]{2,1,0:T(8,128)(2,1)S(1)}, bf16[2,32,2560]{2,1,0:T(8,128)(2,1)S(1)}, bf16[2,16,2560]{2,1,0:T(8,128)(2,1)S(1)}, bf16[2,16,2560]{2,1,0:T...) custom-call(s32[2]{0:T(128)S(1)} %pad_add_fusion.where_ref, ...), custom_call_target="tpu_custom_call" | custom-call | tf_op jit(solution)/shard_map/pack/pallas_call | solution.py:267
  4.8 3.0 %collective-permute-start.6 = (bf16[2,32,2560]{2,1,0:T(8,128)(2,1)S(1)}, bf16[2,32,2560]{2,1,0:T(8,128)(2,1)S(1)}, u32[]{:S(2)}, u32[]{:S(2)}) collective-permute-start(bf16[2,32,2560]{2,1,0:T(8,128)(2,1)S(1)} %get-tuple-element.37), channel_id=1, source_target_pairs={{0,1},{1,2},{2,3},{3,0},{4,5},{5,6},{6,7},{7,4},{8,9},{9,10},{10,1... | collective-permute-start | bytes 983048 | tf_op jit(solution)/shard_map/ppermute | solution.py:30
  7.9 2.6 %collective-permute-start.10 = (bf16[2,16,2560]{2,1,0:T(8,128)(2,1)S(1)}, bf16[2,16,2560]{2,1,0:T(8,128)(2,1)S(1)}, u32[]{:S(2)}, u32[]{:S(2)}) collective-permute-start(bf16[2,16,2560]{2,1,0:T(8,128)(2,1)S(1)} %get-tuple-element.40), channel_id=1, source_target_pairs={{0,2},{1,3},{2,0},{3,1},{4,6},{5,7},{6,4},{7,5},{8,10},{9,11},{10,... | collective-permute-start | bytes 491528 | tf_op jit(solution)/shard_map/ppermute | solution.py:30
  10.8 17.7 %collective-permute-done.10.refs_0_.refs_8_ = bf16[2,16,2560]{2,1,0:T(8,128)(2,1)S(1)} collective-permute-done((bf16[2,16,2560]{2,1,0:T(8,128)(2,1)S(1)}, bf16[2,16,2560]{2,1,0:T(8,128)(2,1)S(1)}, u32[]{:S(2)}, u32[]{:S(2)}) %collective-permute-start.10) | collective-permute-done | bytes 163872 | tf_op jit(solution)/shard_map/ppermute | solution.py:30
  28.5 2.4 %collective-permute-start.16 = (bf16[2,16,2560]{2,1,0:T(8,128)(2,1)S(1)}, bf16[2,16,2560]{2,1,0:T(8,128)(2,1)S(1)}, u32[]{:S(2)}, u32[]{:S(2)}) collective-permute-start(bf16[2,16,2560]{2,1,0:T(8,128)(2,1)S(1)} %get-tuple-element.44), channel_id=1, source_target_pairs={{0,3},{1,0},{2,1},{3,2},{4,7},{5,4},{6,5},{7,6},{8,11},{9,8},{10,9... | collective-permute-start | bytes 491528 | tf_op jit(solution)/shard_map/ppermute | solution.py:30
  30.9 1.1 collective-permute-done.12.refs_2_.refs_10_
  32.0 1.5 %collective-permute-start.1 = (bf16[2,32,2560]{2,1,0:T(8,128)(2,1)S(1)}, bf16[2,32,2560]{2,1,0:T(8,128)(2,1)S(1)}, u32[]{:S(2)}, u32[]{:S(2)}) collective-permute-start(bf16[2,32,2560]{2,1,0:T(8,128)(2,1)S(1)} %get-tuple-element.32.refs_0_.refs_4_), channel_id=1, source_target_pairs={{0,8},{1,9},{2,10},{3,11},{4,12},{5,13},{6,14},{7,15},{8,0},{9,1},... | collective-permute-start | bytes 983048 | tf_op jit(solution)/shard_map/ppermute | solution.py:30
  34.0 1.4 %collective-permute-done.16.refs_0_.refs_12_ = bf16[2,16,2560]{2,1,0:T(8,128)(2,1)S(1)} collective-permute-done((bf16[2,16,2560]{2,1,0:T(8,128)(2,1)S(1)}, bf16[2,16,2560]{2,1,0:T(8,128)(2,1)S(1)}, u32[]{:S(2)}, u32[]{:S(2)}) %collective-permute-start.16) | collective-permute-done | bytes 163872 | tf_op jit(solution)/shard_map/ppermute | solution.py:30
  35.4 2.6 %collective-permute-start.18 = (bf16[2,16,2560]{2,1,0:T(8,128)(2,1)S(1)}, bf16[2,16,2560]{2,1,0:T(8,128)(2,1)S(1)}, u32[]{:S(2)}, u32[]{:S(2)}) collective-permute-start(bf16[2,16,2560]{2,1,0:T(8,128)(2,1)S(1)} %get-tuple-element.45), channel_id=1, source_target_pairs={{0,3},{1,0},{2,1},{3,2},{4,7},{5,4},{6,5},{7,6},{8,11},{9,8},{10,9... | collective-permute-start | bytes 491528 | tf_op jit(solution)/shard_map/ppermute | solution.py:30
  38.0 3.5 %collective-permute-done.18.refs_2_.refs_14_ = bf16[2,16,2560]{2,1,0:T(8,128)(2,1)S(1)} collective-permute-done((bf16[2,16,2560]{2,1,0:T(8,128)(2,1)S(1)}, bf16[2,16,2560]{2,1,0:T(8,128)(2,1)S(1)}, u32[]{:S(2)}, u32[]{:S(2)}) %collective-permute-start.18) | collective-permute-done | bytes 163872 | tf_op jit(solution)/shard_map/ppermute | solution.py:30
  41.5 1.5 %collective-permute-start.11 = (bf16[2,16,2560]{2,1,0:T(8,128)(2,1)S(1)}, bf16[2,16,2560]{2,1,0:T(8,128)(2,1)S(1)}, u32[]{:S(2)}, u32[]{:S(2)}) collective-permute-start(bf16[2,16,2560]{2,1,0:T(8,128)(2,1)S(1)} %collective-permute-done.10.refs_0_.refs_8_), channel_id=1, source_target_pairs={{0,8},{1,9},{2,10},{3,11},{4,12},{5,13},{6,14},{7,15},{8,0},{9,1},... | collective-permute-start | bytes 491528 | tf_op jit(solution)/shard_map/ppermute | solution.py:30
  43.0 1.1 collective-permute-start.13
  44.1 2.1 %fetch.1 = (bf16[2,256,2560]{2,1,0:T(8,128)(2,1)S(1)}, bf16[256,2560]{1,0:T(8,128)(2,1)S(1)}) custom-call(bf16[2,256,2560]{2,1,0:T(8,128)(2,1)} %bitcast.16, bf16[256,2560]{1,0:T(8,128)(2,1)} %bitcast.19), custom_call_target="tpu_custom_call" | custom-call | tf_op jit(solution)/shard_map/fetch/pallas_call | solution.py:290
  46.3 1.0 collective-permute-start.17
  47.3 1.1 collective-permute-start.19
  48.4 4.4 %shard_map.93 = (f32[32,2560]{1,0:T(8,128)S(1)}, bf16[32,2560]{1,0:T(8,128)(2,1)S(1)}, bf16[64,768]{1,0:T(8,128)(2,1)S(1)}, bf16[64,5888]{1,0:T(8,128)(2,1)S(1)}) custom-call(s32[2]{0:T(128)S(1)} %pad_add_fusion.where_ref, bf16[2,32,2560]{2,1,0:T(8,128)(2,1)S(1)} %get-tuple-element.32.refs_0_.refs_4_, ...), custom_call_target="tpu_custom_call" | custom-call | tf_op jit(solution)/shard_map/pallas_call | solution.py:42
  52.7 1.0 collective-permute-start.4
  53.7 4.4 %shard_map.94 = (f32[32,2560]{1,0:T(8,128)S(1)}, bf16[32,2560]{1,0:T(8,128)(2,1)S(1)}, bf16[64,768]{1,0:T(8,128)(2,1)S(1)}, bf16[64,5888]{1,0:T(8,128)(2,1)S(1)}) custom-call(s32[2]{0:T(128)S(1)} %pad_add_fusion.where_ref, bf16[2,32,2560]{2,1,0:T(8,128)(2,1)S(1)} %collective-permute-done.6.refs_0_.refs_6_, ...), custom_call_target="tpu_custom_call" | custom-call | tf_op jit(solution)/shard_map/pallas_call | solution.py:42
  58.1 2.4 %collective-permute-start = (f32[2,128]{1,0:T(2,128)S(1)}, f32[2,128]{1,0:T(2,128)S(1)}, u32[]{:S(2)}, u32[]{:S(2)}) collective-permute-start(f32[2,128]{1,0:T(2,128)S(1)} %bitcast.13), channel_id=1, source_target_pairs={{0,16},{1,17},{2,18},{3,19},{4,20},{5,21},{6,22},{7,23},{8,24},{9,... | collective-permute-start | bytes 3080 | tf_op jit(solution)/shard_map/ppermute | solution.py:30
  60.6 1.1 collective-permute-start.8
  61.7 4.4 %shard_map.95 = (f32[32,2560]{1,0:T(8,128)S(1)}, bf16[32,2560]{1,0:T(8,128)(2,1)S(1)}, bf16[64,768]{1,0:T(8,128)(2,1)S(1)}, bf16[64,5888]{1,0:T(8,128)(2,1)S(1)}) custom-call(s32[2]{0:T(128)S(1)} %pad_add_fusion.where_ref, bf16[2,16,2560]{2,1,0:T(8,128)(2,1)S(1)} %collective-permute-done.10.refs_0_.refs_8_, ...), custom_call_target="tpu_custom_call" | custom-call | tf_op jit(solution)/shard_map/pallas_call | solution.py:42
  66.1 1.0 collective-permute-start.14
  67.1 4.4 %shard_map.96 = (f32[32,2560]{1,0:T(8,128)S(1)}, bf16[32,2560]{1,0:T(8,128)(2,1)S(1)}, bf16[64,768]{1,0:T(8,128)(2,1)S(1)}, bf16[64,5888]{1,0:T(8,128)(2,1)S(1)}) custom-call(s32[2]{0:T(128)S(1)} %pad_add_fusion.where_ref, bf16[2,16,2560]{2,1,0:T(8,128)(2,1)S(1)} %collective-permute-done.16.refs_0_.refs_12_, ...), custom_call_target="tpu_custom_call" | custom-call | tf_op jit(solution)/shard_map/pallas_call | solution.py:42
  71.4 1.2 %collective-permute-start.20 = (bf16[32,2560]{1,0:T(8,128)(2,1)S(1)}, bf16[32,2560]{1,0:T(8,128)(2,1)S(1)}, u32[]{:S(2)}, u32[]{:S(2)}) collective-permute-start(bf16[32,2560]{1,0:T(8,128)(2,1)S(1)} %get-tuple-element.47), channel_id=1, source_target_pairs={{0,8},{1,9},{2,10},{3,11},{4,12},{5,13},{6,14},{7,15},{8,0},{9,1},... | collective-permute-start | bytes 491528 | tf_op jit(solution)/shard_map/ppermute | solution.py:30
  72.7 1.0 collective-permute-start.5
  74.2 3.2 %collective-permute-start.9 = (bf16[32,2560]{1,0:T(8,128)(2,1)S(1)}, bf16[32,2560]{1,0:T(8,128)(2,1)S(1)}, u32[]{:S(2)}, u32[]{:S(2)}) collective-permute-start(bf16[32,2560]{1,0:T(8,128)(2,1)S(1)} %add_convert_fusion.2), channel_id=1, source_target_pairs={{0,19},{1,16},{2,17},{3,18},{4,23},{5,20},{6,21},{7,22},{8,27},{9,... | collective-permute-start | bytes 491528 | tf_op jit(solution)/shard_map/ppermute | solution.py:30
  78.0 4.9 %collective-permute-done.5.refs_0_ = bf16[32,2560]{1,0:T(8,128)(2,1)S(1)} collective-permute-done((bf16[32,2560]{1,0:T(8,128)(2,1)S(1)}, bf16[32,2560]{1,0:T(8,128)(2,1)S(1)}, u32[]{:S(2)}, u32[]{:S(2)}) %collective-permute-start.5) | collective-permute-done | bytes 163872 | tf_op jit(solution)/shard_map/ppermute | solution.py:30
  83.1 11.1 %collective-permute-done.15.refs_2_ = bf16[32,2560]{1,0:T(8,128)(2,1)S(1)} collective-permute-done((bf16[32,2560]{1,0:T(8,128)(2,1)S(1)}, bf16[32,2560]{1,0:T(8,128)(2,1)S(1)}, u32[]{:S(2)}, u32[]{:S(2)}) %collective-permute-start.15) | collective-permute-done | bytes 163872 | tf_op jit(solution)/shard_map/ppermute | solution.py:30
  94.2 8.9 %collective-permute-done.21.refs_3_ = bf16[32,2560]{1,0:T(8,128)(2,1)S(1)} collective-permute-done((bf16[32,2560]{1,0:T(8,128)(2,1)S(1)}, bf16[32,2560]{1,0:T(8,128)(2,1)S(1)}, u32[]{:S(2)}, u32[]{:S(2)}) %collective-permute-start.21) | collective-permute-done | bytes 163872 | tf_op jit(solution)/shard_map/ppermute | solution.py:30
  103.1 2.0 %shard_map.97 = (bf16[128,2560]{1,0:T(8,128)(2,1)}, bf16[128,2560]{1,0:T(8,128)(2,1)}) custom-call(s32[2]{0:T(128)S(1)} %pad_add_fusion.where_ref, f32[2,128]{1,0:T(2,128)S(1)} %collective-permute-done.info, bf16[32,2560]{1,0:T(8,128)(2,1)S(1)} %collective-permute-done.5.refs_0_, bf16[32,2560]{1,0:T(8,128)(2,1)S(1)} %collective-permute-done.9.refs_1_, ...), custom_call_target="tpu_custom_call" | custom-call | tf_op jit(solution)/shard_map/pallas_call | solution.py:42
  105.1 3.1 %shard_map.98 = bf16[2,256,2560]{2,1,0:T(8,128)(2,1)} custom-call(bf16[64,768]{1,0:T(8,128)(2,1)S(1)} %get-tuple-element.50.refs_0_, bf16[64,768]{1,0:T(8,128)(2,1)S(1)} %get-tuple-element.51.refs_1_, bf16[64,768]{1,0:T(8,128)(2,1)S(1)} %get-tuple-element.52.refs_2_, bf16[64,768]{1,0:T(8,128)(2,1)S(1)} %get-tuple-element.53.refs_3_, ...), custom_call_target="tpu_custom_call" | custom-call | tf_op jit(solution)/shard_map/pallas_call | solution.py:42
  108.2 1.9 %shard_map.99 = bf16[1,256,2560]{2,1,0:T(8,128)(2,1)} custom-call(bf16[64,768]{1,0:T(8,128)(2,1)S(1)} %get-tuple-element.50.refs_0_, bf16[64,768]{1,0:T(8,128)(2,1)S(1)} %get-tuple-element.51.refs_1_, bf16[64,768]{1,0:T(8,128)(2,1)S(1)} %get-tuple-element.52.refs_2_, bf16[64,768]{1,0:T(8,128)(2,1)S(1)} %get-tuple-element.53.refs_3_, ...), custom_call_target="tpu_custom_call" | custom-call | tf_op jit(solution)/shard_map/pallas_call | solution.py:42
  (34 shorter events, 3.0 us)
Async XLA Ops:
  0.6 46.6 %collective-permute-start.2 = (bf16[2,256,2560]{2,1,0:T(8,128)(2,1)}, bf16[2,256,2560]{2,1,0:T(8,128)(2,1)S(1)}, u32[]{:S(2)}, u32[]{:S(2)}) collective-permute-start(bf16[2,256,2560]{2,1,0:T(8,128)(2,1)} %bitcast.15), channel_id=1, source_target_pairs={{0,4},{1,5},{2,6},{3,7},{4,0},{5,1},{6,2},{7,3},{8,12},{9,13},{10,... | collective-permute-start | bytes 7864328 | tf_op jit(solution)/shard_map/ppermute | solution.py:30
  1.2 45.1 %collective-permute-start.3 = (bf16[256,2560]{1,0:T(8,128)(2,1)}, bf16[256,2560]{1,0:T(8,128)(2,1)}, u32[]{:S(2)}, u32[]{:S(2)}) collective-permute-start(bf16[256,2560]{1,0:T(8,128)(2,1)} %bitcast.18), channel_id=1, source_target_pairs={{0,4},{1,5},{2,6},{3,7},{4,0},{5,1},{6,2},{7,3},{8,12},{9,13},{10,... | collective-permute-start | bytes 3932168 | tf_op jit(solution)/shard_map/ppermute | solution.py:30
  4.8 28.7 %collective-permute-start.6 = (bf16[2,32,2560]{2,1,0:T(8,128)(2,1)S(1)}, bf16[2,32,2560]{2,1,0:T(8,128)(2,1)S(1)}, u32[]{:S(2)}, u32[]{:S(2)}) collective-permute-start(bf16[2,32,2560]{2,1,0:T(8,128)(2,1)S(1)} %get-tuple-element.37), channel_id=1, source_target_pairs={{0,1},{1,2},{2,3},{3,0},{4,5},{5,6},{6,7},{7,4},{8,9},{9,10},{10,1... | collective-permute-start | bytes 983048 | tf_op jit(solution)/shard_map/ppermute | solution.py:30
  7.9 20.6 %collective-permute-start.10 = (bf16[2,16,2560]{2,1,0:T(8,128)(2,1)S(1)}, bf16[2,16,2560]{2,1,0:T(8,128)(2,1)S(1)}, u32[]{:S(2)}, u32[]{:S(2)}) collective-permute-start(bf16[2,16,2560]{2,1,0:T(8,128)(2,1)S(1)} %get-tuple-element.40), channel_id=1, source_target_pairs={{0,2},{1,3},{2,0},{3,1},{4,6},{5,7},{6,4},{7,5},{8,10},{9,11},{10,... | collective-permute-start | bytes 491528 | tf_op jit(solution)/shard_map/ppermute | solution.py:30
  10.5 21.5 %collective-permute-start.12 = (bf16[2,16,2560]{2,1,0:T(8,128)(2,1)S(1)}, bf16[2,16,2560]{2,1,0:T(8,128)(2,1)S(1)}, u32[]{:S(2)}, u32[]{:S(2)}) collective-permute-start(bf16[2,16,2560]{2,1,0:T(8,128)(2,1)S(1)} %get-tuple-element.41), channel_id=1, source_target_pairs={{0,2},{1,3},{2,0},{3,1},{4,6},{5,7},{6,4},{7,5},{8,10},{9,11},{10,... | collective-permute-start | bytes 491528 | tf_op jit(solution)/shard_map/ppermute | solution.py:30
  28.5 6.9 %collective-permute-start.16 = (bf16[2,16,2560]{2,1,0:T(8,128)(2,1)S(1)}, bf16[2,16,2560]{2,1,0:T(8,128)(2,1)S(1)}, u32[]{:S(2)}, u32[]{:S(2)}) collective-permute-start(bf16[2,16,2560]{2,1,0:T(8,128)(2,1)S(1)} %get-tuple-element.44), channel_id=1, source_target_pairs={{0,3},{1,0},{2,1},{3,2},{4,7},{5,4},{6,5},{7,6},{8,11},{9,8},{10,9... | collective-permute-start | bytes 491528 | tf_op jit(solution)/shard_map/ppermute | solution.py:30
  32.0 11.0 %collective-permute-start.1 = (bf16[2,32,2560]{2,1,0:T(8,128)(2,1)S(1)}, bf16[2,32,2560]{2,1,0:T(8,128)(2,1)S(1)}, u32[]{:S(2)}, u32[]{:S(2)}) collective-permute-start(bf16[2,32,2560]{2,1,0:T(8,128)(2,1)S(1)} %get-tuple-element.32.refs_0_.refs_4_), channel_id=1, source_target_pairs={{0,8},{1,9},{2,10},{3,11},{4,12},{5,13},{6,14},{7,15},{8,0},{9,1},... | collective-permute-start | bytes 983048 | tf_op jit(solution)/shard_map/ppermute | solution.py:30
  33.5 19.2 %collective-permute-start.7 = (bf16[2,32,2560]{2,1,0:T(8,128)(2,1)S(1)}, bf16[2,32,2560]{2,1,0:T(8,128)(2,1)S(1)}, u32[]{:S(2)}, u32[]{:S(2)}) collective-permute-start(bf16[2,32,2560]{2,1,0:T(8,128)(2,1)S(1)} %collective-permute-done.6.refs_0_.refs_6_), channel_id=1, source_target_pairs={{0,8},{1,9},{2,10},{3,11},{4,12},{5,13},{6,14},{7,15},{8,0},{9,1},... | collective-permute-start | bytes 983048 | tf_op jit(solution)/shard_map/ppermute | solution.py:30
  35.4 6.1 %collective-permute-start.18 = (bf16[2,16,2560]{2,1,0:T(8,128)(2,1)S(1)}, bf16[2,16,2560]{2,1,0:T(8,128)(2,1)S(1)}, u32[]{:S(2)}, u32[]{:S(2)}) collective-permute-start(bf16[2,16,2560]{2,1,0:T(8,128)(2,1)S(1)} %get-tuple-element.45), channel_id=1, source_target_pairs={{0,3},{1,0},{2,1},{3,2},{4,7},{5,4},{6,5},{7,6},{8,11},{9,8},{10,9... | collective-permute-start | bytes 491528 | tf_op jit(solution)/shard_map/ppermute | solution.py:30
  41.5 16.6 %collective-permute-start.11 = (bf16[2,16,2560]{2,1,0:T(8,128)(2,1)S(1)}, bf16[2,16,2560]{2,1,0:T(8,128)(2,1)S(1)}, u32[]{:S(2)}, u32[]{:S(2)}) collective-permute-start(bf16[2,16,2560]{2,1,0:T(8,128)(2,1)S(1)} %collective-permute-done.10.refs_0_.refs_8_), channel_id=1, source_target_pairs={{0,8},{1,9},{2,10},{3,11},{4,12},{5,13},{6,14},{7,15},{8,0},{9,1},... | collective-permute-start | bytes 491528 | tf_op jit(solution)/shard_map/ppermute | solution.py:30
  43.0 17.6 %collective-permute-start.13 = (bf16[2,16,2560]{2,1,0:T(8,128)(2,1)S(1)}, bf16[2,16,2560]{2,1,0:T(8,128)(2,1)S(1)}, u32[]{:S(2)}, u32[]{:S(2)}) collective-permute-start(bf16[2,16,2560]{2,1,0:T(8,128)(2,1)S(1)} %collective-permute-done.12.refs_2_.refs_10_), channel_id=1, source_target_pairs={{0,8},{1,9},{2,10},{3,11},{4,12},{5,13},{6,14},{7,15},{8,0},{9,1},... | collective-permute-start | bytes 491528 | tf_op jit(solution)/shard_map/ppermute | solution.py:30
  46.3 19.8 %collective-permute-start.17 = (bf16[2,16,2560]{2,1,0:T(8,128)(2,1)S(1)}, bf16[2,16,2560]{2,1,0:T(8,128)(2,1)S(1)}, u32[]{:S(2)}, u32[]{:S(2)}) collective-permute-start(bf16[2,16,2560]{2,1,0:T(8,128)(2,1)S(1)} %collective-permute-done.16.refs_0_.refs_12_), channel_id=1, source_target_pairs={{0,8},{1,9},{2,10},{3,11},{4,12},{5,13},{6,14},{7,15},{8,0},{9,1},... | collective-permute-start | bytes 491528 | tf_op jit(solution)/shard_map/ppermute | solution.py:30
  47.3 19.8 %collective-permute-start.19 = (bf16[2,16,2560]{2,1,0:T(8,128)(2,1)S(1)}, bf16[2,16,2560]{2,1,0:T(8,128)(2,1)S(1)}, u32[]{:S(2)}, u32[]{:S(2)}) collective-permute-start(bf16[2,16,2560]{2,1,0:T(8,128)(2,1)S(1)} %collective-permute-done.18.refs_2_.refs_14_), channel_id=1, source_target_pairs={{0,8},{1,9},{2,10},{3,11},{4,12},{5,13},{6,14},{7,15},{8,0},{9,1},... | collective-permute-start | bytes 491528 | tf_op jit(solution)/shard_map/ppermute | solution.py:30
  52.7 19.9 %collective-permute-start.4 = (bf16[32,2560]{1,0:T(8,128)(2,1)S(1)}, bf16[32,2560]{1,0:T(8,128)(2,1)S(1)}, u32[]{:S(2)}, u32[]{:S(2)}) collective-permute-start(bf16[32,2560]{1,0:T(8,128)(2,1)S(1)} %get-tuple-element.36), channel_id=1, source_target_pairs={{0,8},{1,9},{2,10},{3,11},{4,12},{5,13},{6,14},{7,15},{8,0},{9,1},... | collective-permute-start | bytes 491528 | tf_op jit(solution)/shard_map/ppermute | solution.py:30
  58.1 19.3 %collective-permute-start = (f32[2,128]{1,0:T(2,128)S(1)}, f32[2,128]{1,0:T(2,128)S(1)}, u32[]{:S(2)}, u32[]{:S(2)}) collective-permute-start(f32[2,128]{1,0:T(2,128)S(1)} %bitcast.13), channel_id=1, source_target_pairs={{0,16},{1,17},{2,18},{3,19},{4,20},{5,21},{6,22},{7,23},{8,24},{9,... | collective-permute-start | bytes 3080 | tf_op jit(solution)/shard_map/ppermute | solution.py:30
  60.6 12.1 %collective-permute-start.8 = (bf16[32,2560]{1,0:T(8,128)(2,1)S(1)}, bf16[32,2560]{1,0:T(8,128)(2,1)S(1)}, u32[]{:S(2)}, u32[]{:S(2)}) collective-permute-start(bf16[32,2560]{1,0:T(8,128)(2,1)S(1)} %get-tuple-element.39), channel_id=1, source_target_pairs={{0,8},{1,9},{2,10},{3,11},{4,12},{5,13},{6,14},{7,15},{8,0},{9,1},... | collective-permute-start | bytes 491528 | tf_op jit(solution)/shard_map/ppermute | solution.py:30
  66.1 8.1 %collective-permute-start.14 = (bf16[32,2560]{1,0:T(8,128)(2,1)S(1)}, bf16[32,2560]{1,0:T(8,128)(2,1)S(1)}, u32[]{:S(2)}, u32[]{:S(2)}) collective-permute-start(bf16[32,2560]{1,0:T(8,128)(2,1)S(1)} %get-tuple-element.43), channel_id=1, source_target_pairs={{0,8},{1,9},{2,10},{3,11},{4,12},{5,13},{6,14},{7,15},{8,0},{9,1},... | collective-permute-start | bytes 491528 | tf_op jit(solution)/shard_map/ppermute | solution.py:30
  71.4 6.0 %collective-permute-start.20 = (bf16[32,2560]{1,0:T(8,128)(2,1)S(1)}, bf16[32,2560]{1,0:T(8,128)(2,1)S(1)}, u32[]{:S(2)}, u32[]{:S(2)}) collective-permute-start(bf16[32,2560]{1,0:T(8,128)(2,1)S(1)} %get-tuple-element.47), channel_id=1, source_target_pairs={{0,8},{1,9},{2,10},{3,11},{4,12},{5,13},{6,14},{7,15},{8,0},{9,1},... | collective-permute-start | bytes 491528 | tf_op jit(solution)/shard_map/ppermute | solution.py:30
  72.6 32.5 %collective-permute-start.22 = (bf16[64,5888]{1,0:T(8,128)(2,1)S(1)}, bf16[64,5888]{1,0:T(8,128)(2,1)S(1)}, u32[]{:S(2)}, u32[]{:S(2)}) collective-permute-start(bf16[64,5888]{1,0:T(8,128)(2,1)S(1)} %get-tuple-element.54), channel_id=1, source_target_pairs={{0,4},{1,5},{2,6},{3,7},{4,0},{5,1},{6,2},{7,3},{8,12},{9,13},{10,... | collective-permute-start | bytes 2261000 | tf_op jit(solution)/shard_map/ppermute | solution.py:30
  72.7 10.2 %collective-permute-start.5 = (bf16[32,2560]{1,0:T(8,128)(2,1)S(1)}, bf16[32,2560]{1,0:T(8,128)(2,1)S(1)}, u32[]{:S(2)}, u32[]{:S(2)}) collective-permute-start(bf16[32,2560]{1,0:T(8,128)(2,1)S(1)} %add_convert_fusion.3), channel_id=1, source_target_pairs={{0,16},{1,17},{2,18},{3,19},{4,20},{5,21},{6,22},{7,23},{8,24},{9,... | collective-permute-start | bytes 491528 | tf_op jit(solution)/shard_map/ppermute | solution.py:30
  74.2 8.7 %collective-permute-start.9 = (bf16[32,2560]{1,0:T(8,128)(2,1)S(1)}, bf16[32,2560]{1,0:T(8,128)(2,1)S(1)}, u32[]{:S(2)}, u32[]{:S(2)}) collective-permute-start(bf16[32,2560]{1,0:T(8,128)(2,1)S(1)} %add_convert_fusion.2), channel_id=1, source_target_pairs={{0,19},{1,16},{2,17},{3,18},{4,23},{5,20},{6,21},{7,22},{8,27},{9,... | collective-permute-start | bytes 491528 | tf_op jit(solution)/shard_map/ppermute | solution.py:30
  77.4 27.7 %collective-permute-start.23 = (bf16[64,5888]{1,0:T(8,128)(2,1)S(1)}, bf16[64,5888]{1,0:T(8,128)(2,1)S(1)}, u32[]{:S(2)}, u32[]{:S(2)}) collective-permute-start(bf16[64,5888]{1,0:T(8,128)(2,1)S(1)} %get-tuple-element.55), channel_id=1, source_target_pairs={{0,4},{1,5},{2,6},{3,7},{4,0},{5,1},{6,2},{7,3},{8,12},{9,13},{10,... | collective-permute-start | bytes 2261000 | tf_op jit(solution)/shard_map/ppermute | solution.py:30
  77.5 27.6 %collective-permute-start.24 = (bf16[64,5888]{1,0:T(8,128)(2,1)S(1)}, bf16[64,5888]{1,0:T(8,128)(2,1)S(1)}, u32[]{:S(2)}, u32[]{:S(2)}) collective-permute-start(bf16[64,5888]{1,0:T(8,128)(2,1)S(1)} %get-tuple-element.56), channel_id=1, source_target_pairs={{0,4},{1,5},{2,6},{3,7},{4,0},{5,1},{6,2},{7,3},{8,12},{9,13},{10,... | collective-permute-start | bytes 2261000 | tf_op jit(solution)/shard_map/ppermute | solution.py:30
  82.8 22.2 %collective-permute-start.25 = (bf16[64,5888]{1,0:T(8,128)(2,1)S(1)}, bf16[64,5888]{1,0:T(8,128)(2,1)S(1)}, u32[]{:S(2)}, u32[]{:S(2)}) collective-permute-start(bf16[64,5888]{1,0:T(8,128)(2,1)S(1)} %get-tuple-element.57), channel_id=1, source_target_pairs={{0,4},{1,5},{2,6},{3,7},{4,0},{5,1},{6,2},{7,3},{8,12},{9,13},{10,... | collective-permute-start | bytes 2261000 | tf_op jit(solution)/shard_map/ppermute | solution.py:30
  82.8 11.4 %collective-permute-start.15 = (bf16[32,2560]{1,0:T(8,128)(2,1)S(1)}, bf16[32,2560]{1,0:T(8,128)(2,1)S(1)}, u32[]{:S(2)}, u32[]{:S(2)}) collective-permute-start(bf16[32,2560]{1,0:T(8,128)(2,1)S(1)} %add_convert_fusion.1), channel_id=1, source_target_pairs={{0,18},{1,19},{2,16},{3,17},{4,22},{5,23},{6,20},{7,21},{8,26},{9,... | collective-permute-start | bytes 491528 | tf_op jit(solution)/shard_map/ppermute | solution.py:30
  94.2 8.9 %collective-permute-start.21 = (bf16[32,2560]{1,0:T(8,128)(2,1)S(1)}, bf16[32,2560]{1,0:T(8,128)(2,1)S(1)}, u32[]{:S(2)}, u32[]{:S(2)}) collective-permute-start(bf16[32,2560]{1,0:T(8,128)(2,1)S(1)} %add_convert_fusion), channel_id=1, source_target_pairs={{0,17},{1,18},{2,19},{3,16},{4,21},{5,22},{6,23},{7,20},{8,25},{9,... | collective-permute-start | bytes 491528 | tf_op jit(solution)/shard_map/ppermute | solution.py:30
where the time goes:
time: 110 us
  waiting for transfers between devices  49 us (45%)
  starting transfers between devices  30.1 us (27%)
  Pallas kernels  30.1 us (27%)
    ppermute x26, waiting for transfers between devices, moved(): return lax.ppermute(value, AXES, pairs)  49 us
    ppermute x26, starting transfers between devices, moved(): return lax.ppermute(value, AXES, pairs)  30.1 us
    pallas_call x7, Pallas kernels, call(): pl.pallas_call(body, out_shape=outs, in_specs=[IN_SMEM] * smem + [IN_VMEM...  24.5 us
    pallas_call x1, Pallas kernels, computed(): pl.pallas_call(functools.partial(pack_body, window, units, lanes), out_sh...  3.49 us
  transfers between devices with their start and end apart: 26, of which 8 were waited for; matrix products, arithmetic and copies ran while one was open for 0% of the time, Pallas kernels for 23%

commit v1 on v0

--- a/solution.py
+++ b/solution.py
@@ -141,9 +141,9 @@
     rows, grads = bundle[:, :width], bundle[:, width : 2 * width]
     sent = bundle.at[:, 2 * width :]
     for gate_up, down, hidden_out in ((gate_up_here, down_here, kept), (gate_up_pair, down_pair, sent)):
-        pre_gate = dot(rows, gate_up[0], LAST)
-        pre_up = dot(rows, gate_up[1], LAST)
-        hidden_grad = dot(grads, down[...], LAST)
+        pre_gate = dot(gate_up[0], rows, LAST).T
+        pre_up = dot(gate_up[1], rows, LAST).T
+        hidden_grad = dot(down[...], grads, LAST).T
         sigmoid = jax.nn.sigmoid(pre_gate)
         activated = pre_gate * sigmoid
         slope = sigmoid * (1.0 + pre_gate * (1.0 - sigmoid))
@@ -207,20 +207,48 @@
         out[i] = value.astype(out.dtype)
 
 
-def final_body(mode, returns, where_ref, info, *refs):
+def final_body(mode, returns, blocks, where_ref, info, *refs):
     section = where_ref[0]
-    sorted_refs = [refs[r] for r in sorted(range(len(returns)), key=lambda r: returns[r])]
-    rows = jnp.concatenate([ref[...] for ref in sorted_refs])
-    outs = refs[len(returns) :]
+    count = len(returns)
+    slots = [refs[r] for r in sorted(range(count), key=lambda r: returns[r])]
+    outs, (value, zero, sems) = refs[count : count + len(mode)], refs[count + len(mode) :]
+    rows_here, width = value.shape
+    step = width // blocks
     place, scale = info[0:1], info[1:2]
-    size = (rows.shape[0], place.shape[1])
-    pick = jnp.where(lax.broadcasted_iota(jnp.int32, size, 0).astype(jnp.float32) == place, 1.0, 0.0)
-    value = dot(pick.astype(jnp.bfloat16), rows, FIRST) * column_of(scale)
-    value = value.astype(jnp.bfloat16)
-    zero = jnp.zeros_like(value)
-    for out, (lowest, highest) in zip(outs, mode):
-        keep = (section >= lowest) & (section <= highest)
-        out[...] = jnp.where(keep, value, zero)
+    pick = jnp.where(
+        lax.broadcasted_iota(jnp.int32, (rows_here, rows_here), 0).astype(jnp.float32) == place, 1.0, 0.0
+    ).astype(jnp.bfloat16)
+    scale_column = column_of(scale)
+
+    def write(target, others):
+        copies = []
+        if others:
+            zero[...] = jnp.zeros_like(zero)
+        for i, other in enumerate(others):
+            copies.append(pltpu.make_async_copy(zero, other, sems.at[blocks + i]))
+            copies[-1].start()
+        for b in range(blocks):
+            at = slice(b * step, (b + 1) * step)
+            rows = jnp.concatenate([ref[:, at] for ref in slots])
+            value[:, at] = (dot(pick, rows, FIRST) * scale_column).astype(jnp.bfloat16)
+            if target is not None:
+                here = pl.ds(b * step, step)
+                copies.append(pltpu.make_async_copy(value.at[:, here], target.at[:, here], sems.at[b]))
+                copies[-1].start()
+        for copy in copies:
+            copy.wait()
+
+    for i, (lowest, highest) in enumerate(mode):
+
+        @pl.when((section >= lowest) & (section <= highest))
+        def _(i=i):
+            write(outs[i], [out for n, out in enumerate(outs) if n != i])
+
+    if len(mode) == 1:
+
+        @pl.when((section < mode[0][0]) | (section > mode[0][1]))
+        def _():
+            write(None, list(outs))
 
 
 def plan(window, capacity):
@@ -363,12 +391,18 @@
     }
     results = []
     for i, (kind, _) in enumerate(lanes):
-        results += call(
-            functools.partial(final_body, modes[kind], returns),
-            [bf16((rows_here, width))] * len(modes[kind]),
-            (position, infos[i], *returned[i]),
-            12,
-        )
+        count = len(modes[kind])
+        blocks = width // step
+        results += pl.pallas_call(
+            functools.partial(final_body, modes[kind], returns, blocks),
+            out_shape=[bf16((rows_here, width))] * count,
+            in_specs=[IN_SMEM] + [IN_VMEM] * (1 + len(returns)),
+            out_specs=[IN_HBM] * count,
+            scratch_shapes=[pltpu.VMEM((rows_here, width), jnp.bfloat16)] * 2
+            + [pltpu.SemaphoreType.DMA((blocks + count,))],
+            compiler_params=pltpu.CompilerParams(vmem_limit_bytes=12 << 20),
+            name="final",
+        )(position, infos[i], *returned[i])
     return (results[0][None], results[1][None], grad_gate_up[None, None], grad_down[None])
 
 

time: 110 us -> 109 us (level)
  Pallas kernels: 30.1 us -> 29 us
    pallas_call x7 -> x6, Pallas kernels: 24.5 us -> 21.6 us  [call(): pl.pallas_call(body, out_shape=outs, in_specs=[IN_SMEM] * smem + [IN_VMEM...]
    pallas_call x0 -> x1, Pallas kernels: none -> 1.77 us  [computed(): pl.pallas_call(functools.partial(final_body, modes[kind], returns, blocks...]
  transfers between devices with their start and end apart: 26 -> 26, of which waited for: 8 -> 8; matrix products, arithmetic and copies ran while one was open for 0% -> 0% of each run, Pallas kernels for 23% -> 22%
where the time goes in v1:
time: 109 us
  waiting for transfers between devices  49.7 us (46%)
  starting transfers between devices  29.3 us (27%)
  Pallas kernels  29 us (27%)
    ppermute x26, waiting for transfers between devices, moved(): return lax.ppermute(value, AXES, pairs)  49.7 us
    ppermute x26, starting transfers between devices, moved(): return lax.ppermute(value, AXES, pairs)  29.3 us
    pallas_call x6, Pallas kernels, call(): pl.pallas_call(body, out_shape=outs, in_specs=[IN_SMEM] * smem + [IN_VMEM...  21.6 us
    pallas_call x1, Pallas kernels, computed(): pl.pallas_call(functools.partial(pack_body, window, units, lanes), out_sh...  3.49 us
  transfers between devices with their start and end apart: 26, of which 8 were waited for; matrix products, arithmetic and copies ran while one was open for 0% of the time, Pallas kernels for 22%

profile of v1, /device:TPU:0, one launch (start us, length us, event | category | flops | bytes accessed | tf_op | source)
XLA Modules:
  0.0 109.0 jit_solution(2101847835238901920)
XLA Ops:
  1.3 3.5 %pack.1 = (bf16[2,32,2560]{2,1,0:T(8,128)(2,1)S(1)}, bf16[2,32,2560]{2,1,0:T(8,128)(2,1)S(1)}, bf16[2,16,2560]{2,1,0:T(8,128)(2,1)S(1)}, bf16[2,16,2560]{2,1,0:T...) custom-call(s32[2]{0:T(128)S(1)} %pad_add_fusion.where_ref, ...), custom_call_target="tpu_custom_call" | custom-call | tf_op jit(solution)/shard_map/pack/pallas_call | solution.py:295
  4.8 3.0 %collective-permute-start.6 = (bf16[2,32,2560]{2,1,0:T(8,128)(2,1)S(1)}, bf16[2,32,2560]{2,1,0:T(8,128)(2,1)S(1)}, u32[]{:S(2)}, u32[]{:S(2)}) collective-permute-start(bf16[2,32,2560]{2,1,0:T(8,128)(2,1)S(1)} %get-tuple-element.37), channel_id=1, source_target_pairs={{0,1},{1,2},{2,3},{3,0},{4,5},{5,6},{6,7},{7,4},{8,9},{9,10},{10,1... | collective-permute-start | bytes 983048 | tf_op jit(solution)/shard_map/ppermute | solution.py:30
  7.9 2.6 %collective-permute-start.10 = (bf16[2,16,2560]{2,1,0:T(8,128)(2,1)S(1)}, bf16[2,16,2560]{2,1,0:T(8,128)(2,1)S(1)}, u32[]{:S(2)}, u32[]{:S(2)}) collective-permute-start(bf16[2,16,2560]{2,1,0:T(8,128)(2,1)S(1)} %get-tuple-element.40), channel_id=1, source_target_pairs={{0,2},{1,3},{2,0},{3,1},{4,6},{5,7},{6,4},{7,5},{8,10},{9,11},{10,... | collective-permute-start | bytes 491528 | tf_op jit(solution)/shard_map/ppermute | solution.py:30
  10.8 17.7 %collective-permute-done.10.refs_0_.refs_8_ = bf16[2,16,2560]{2,1,0:T(8,128)(2,1)S(1)} collective-permute-done((bf16[2,16,2560]{2,1,0:T(8,128)(2,1)S(1)}, bf16[2,16,2560]{2,1,0:T(8,128)(2,1)S(1)}, u32[]{:S(2)}, u32[]{:S(2)}) %collective-permute-start.10) | collective-permute-done | bytes 163872 | tf_op jit(solution)/shard_map/ppermute | solution.py:30
  28.5 2.4 %collective-permute-start.16 = (bf16[2,16,2560]{2,1,0:T(8,128)(2,1)S(1)}, bf16[2,16,2560]{2,1,0:T(8,128)(2,1)S(1)}, u32[]{:S(2)}, u32[]{:S(2)}) collective-permute-start(bf16[2,16,2560]{2,1,0:T(8,128)(2,1)S(1)} %get-tuple-element.44), channel_id=1, source_target_pairs={{0,3},{1,0},{2,1},{3,2},{4,7},{5,4},{6,5},{7,6},{8,11},{9,8},{10,9... | collective-permute-start | bytes 491528 | tf_op jit(solution)/shard_map/ppermute | solution.py:30
  30.9 1.1 collective-permute-done.12.refs_2_.refs_10_
  32.0 1.5 %collective-permute-start.1 = (bf16[2,32,2560]{2,1,0:T(8,128)(2,1)S(1)}, bf16[2,32,2560]{2,1,0:T(8,128)(2,1)S(1)}, u32[]{:S(2)}, u32[]{:S(2)}) collective-permute-start(bf16[2,32,2560]{2,1,0:T(8,128)(2,1)S(1)} %get-tuple-element.32.refs_0_.refs_4_), channel_id=1, source_target_pairs={{0,8},{1,9},{2,10},{3,11},{4,12},{5,13},{6,14},{7,15},{8,0},{9,1},... | collective-permute-start | bytes 983048 | tf_op jit(solution)/shard_map/ppermute | solution.py:30
  34.0 1.4 %collective-permute-done.16.refs_0_.refs_12_ = bf16[2,16,2560]{2,1,0:T(8,128)(2,1)S(1)} collective-permute-done((bf16[2,16,2560]{2,1,0:T(8,128)(2,1)S(1)}, bf16[2,16,2560]{2,1,0:T(8,128)(2,1)S(1)}, u32[]{:S(2)}, u32[]{:S(2)}) %collective-permute-start.16) | collective-permute-done | bytes 163872 | tf_op jit(solution)/shard_map/ppermute | solution.py:30
  35.4 2.6 %collective-permute-start.18 = (bf16[2,16,2560]{2,1,0:T(8,128)(2,1)S(1)}, bf16[2,16,2560]{2,1,0:T(8,128)(2,1)S(1)}, u32[]{:S(2)}, u32[]{:S(2)}) collective-permute-start(bf16[2,16,2560]{2,1,0:T(8,128)(2,1)S(1)} %get-tuple-element.45), channel_id=1, source_target_pairs={{0,3},{1,0},{2,1},{3,2},{4,7},{5,4},{6,5},{7,6},{8,11},{9,8},{10,9... | collective-permute-start | bytes 491528 | tf_op jit(solution)/shard_map/ppermute | solution.py:30
  38.0 3.5 %collective-permute-done.18.refs_2_.refs_14_ = bf16[2,16,2560]{2,1,0:T(8,128)(2,1)S(1)} collective-permute-done((bf16[2,16,2560]{2,1,0:T(8,128)(2,1)S(1)}, bf16[2,16,2560]{2,1,0:T(8,128)(2,1)S(1)}, u32[]{:S(2)}, u32[]{:S(2)}) %collective-permute-start.18) | collective-permute-done | bytes 163872 | tf_op jit(solution)/shard_map/ppermute | solution.py:30
  41.5 1.5 %collective-permute-start.11 = (bf16[2,16,2560]{2,1,0:T(8,128)(2,1)S(1)}, bf16[2,16,2560]{2,1,0:T(8,128)(2,1)S(1)}, u32[]{:S(2)}, u32[]{:S(2)}) collective-permute-start(bf16[2,16,2560]{2,1,0:T(8,128)(2,1)S(1)} %collective-permute-done.10.refs_0_.refs_8_), channel_id=1, source_target_pairs={{0,8},{1,9},{2,10},{3,11},{4,12},{5,13},{6,14},{7,15},{8,0},{9,1},... | collective-permute-start | bytes 491528 | tf_op jit(solution)/shard_map/ppermute | solution.py:30
  43.0 1.1 %collective-permute-start.13 = (bf16[2,16,2560]{2,1,0:T(8,128)(2,1)S(1)}, bf16[2,16,2560]{2,1,0:T(8,128)(2,1)S(1)}, u32[]{:S(2)}, u32[]{:S(2)}) collective-permute-start(bf16[2,16,2560]{2,1,0:T(8,128)(2,1)S(1)} %collective-permute-done.12.refs_2_.refs_10_), channel_id=1, source_target_pairs={{0,8},{1,9},{2,10},{3,11},{4,12},{5,13},{6,14},{7,15},{8,0},{9,1},... | collective-permute-start | bytes 491528 | tf_op jit(solution)/shard_map/ppermute | solution.py:30
  44.1 2.1 %fetch.1 = (bf16[2,256,2560]{2,1,0:T(8,128)(2,1)S(1)}, bf16[256,2560]{1,0:T(8,128)(2,1)S(1)}) custom-call(bf16[2,256,2560]{2,1,0:T(8,128)(2,1)} %bitcast.16, bf16[256,2560]{1,0:T(8,128)(2,1)} %bitcast.19), custom_call_target="tpu_custom_call" | custom-call | tf_op jit(solution)/shard_map/fetch/pallas_call | solution.py:318
  46.3 1.0 collective-permute-start.17
  47.3 1.1 %collective-permute-start.19 = (bf16[2,16,2560]{2,1,0:T(8,128)(2,1)S(1)}, bf16[2,16,2560]{2,1,0:T(8,128)(2,1)S(1)}, u32[]{:S(2)}, u32[]{:S(2)}) collective-permute-start(bf16[2,16,2560]{2,1,0:T(8,128)(2,1)S(1)} %collective-permute-done.18.refs_2_.refs_14_), channel_id=1, source_target_pairs={{0,8},{1,9},{2,10},{3,11},{4,12},{5,13},{6,14},{7,15},{8,0},{9,1},... | collective-permute-start | bytes 491528 | tf_op jit(solution)/shard_map/ppermute | solution.py:30
  48.4 4.2 %shard_map.93 = (f32[32,2560]{1,0:T(8,128)S(1)}, bf16[32,2560]{1,0:T(8,128)(2,1)S(1)}, bf16[64,768]{1,0:T(8,128)(2,1)S(1)}, bf16[64,5888]{1,0:T(8,128)(2,1)S(1)}) custom-call(s32[2]{0:T(128)S(1)} %pad_add_fusion.where_ref, bf16[2,32,2560]{2,1,0:T(8,128)(2,1)S(1)} %get-tuple-element.32.refs_0_.refs_4_, ...), custom_call_target="tpu_custom_call" | custom-call | tf_op jit(solution)/shard_map/pallas_call | solution.py:42
  53.5 4.1 %shard_map.94 = (f32[32,2560]{1,0:T(8,128)S(1)}, bf16[32,2560]{1,0:T(8,128)(2,1)S(1)}, bf16[64,768]{1,0:T(8,128)(2,1)S(1)}, bf16[64,5888]{1,0:T(8,128)(2,1)S(1)}) custom-call(s32[2]{0:T(128)S(1)} %pad_add_fusion.where_ref, bf16[2,32,2560]{2,1,0:T(8,128)(2,1)S(1)} %collective-permute-done.6.refs_0_.refs_6_, ...), custom_call_target="tpu_custom_call" | custom-call | tf_op jit(solution)/shard_map/pallas_call | solution.py:42
  57.7 2.4 %collective-permute-start = (f32[2,128]{1,0:T(2,128)S(1)}, f32[2,128]{1,0:T(2,128)S(1)}, u32[]{:S(2)}, u32[]{:S(2)}) collective-permute-start(f32[2,128]{1,0:T(2,128)S(1)} %bitcast.13), channel_id=1, source_target_pairs={{0,16},{1,17},{2,18},{3,19},{4,20},{5,21},{6,22},{7,23},{8,24},{9,... | collective-permute-start | bytes 3080 | tf_op jit(solution)/shard_map/ppermute | solution.py:30
  60.1 1.1 %collective-permute-start.8 = (bf16[32,2560]{1,0:T(8,128)(2,1)S(1)}, bf16[32,2560]{1,0:T(8,128)(2,1)S(1)}, u32[]{:S(2)}, u32[]{:S(2)}) collective-permute-start(bf16[32,2560]{1,0:T(8,128)(2,1)S(1)} %get-tuple-element.39), channel_id=1, source_target_pairs={{0,8},{1,9},{2,10},{3,11},{4,12},{5,13},{6,14},{7,15},{8,0},{9,1},... | collective-permute-start | bytes 491528 | tf_op jit(solution)/shard_map/ppermute | solution.py:30
  61.2 4.1 %shard_map.95 = (f32[32,2560]{1,0:T(8,128)S(1)}, bf16[32,2560]{1,0:T(8,128)(2,1)S(1)}, bf16[64,768]{1,0:T(8,128)(2,1)S(1)}, bf16[64,5888]{1,0:T(8,128)(2,1)S(1)}) custom-call(s32[2]{0:T(128)S(1)} %pad_add_fusion.where_ref, bf16[2,16,2560]{2,1,0:T(8,128)(2,1)S(1)} %collective-permute-done.10.refs_0_.refs_8_, ...), custom_call_target="tpu_custom_call" | custom-call | tf_op jit(solution)/shard_map/pallas_call | solution.py:42
  65.4 1.0 collective-permute-start.14
  66.4 4.2 %shard_map.96 = (f32[32,2560]{1,0:T(8,128)S(1)}, bf16[32,2560]{1,0:T(8,128)(2,1)S(1)}, bf16[64,768]{1,0:T(8,128)(2,1)S(1)}, bf16[64,5888]{1,0:T(8,128)(2,1)S(1)}) custom-call(s32[2]{0:T(128)S(1)} %pad_add_fusion.where_ref, bf16[2,16,2560]{2,1,0:T(8,128)(2,1)S(1)} %collective-permute-done.16.refs_0_.refs_12_, ...), custom_call_target="tpu_custom_call" | custom-call | tf_op jit(solution)/shard_map/pallas_call | solution.py:42
  70.5 1.2 %collective-permute-start.20 = (bf16[32,2560]{1,0:T(8,128)(2,1)S(1)}, bf16[32,2560]{1,0:T(8,128)(2,1)S(1)}, u32[]{:S(2)}, u32[]{:S(2)}) collective-permute-start(bf16[32,2560]{1,0:T(8,128)(2,1)S(1)} %get-tuple-element.47), channel_id=1, source_target_pairs={{0,8},{1,9},{2,10},{3,11},{4,12},{5,13},{6,14},{7,15},{8,0},{9,1},... | collective-permute-start | bytes 491528 | tf_op jit(solution)/shard_map/ppermute | solution.py:30
  71.7 1.0 collective-permute-start.5
  72.8 1.4 %collective-permute-done.14 = bf16[32,2560]{1,0:T(8,128)(2,1)S(1)} collective-permute-done((bf16[32,2560]{1,0:T(8,128)(2,1)S(1)}, bf16[32,2560]{1,0:T(8,128)(2,1)S(1)}, u32[]{:S(2)}, u32[]{:S(2)}) %collective-permute-start.14) | collective-permute-done | bytes 163872 | tf_op jit(solution)/shard_map/ppermute | solution.py:30
  74.2 2.5 %collective-permute-start.9 = (bf16[32,2560]{1,0:T(8,128)(2,1)S(1)}, bf16[32,2560]{1,0:T(8,128)(2,1)S(1)}, u32[]{:S(2)}, u32[]{:S(2)}) collective-permute-start(bf16[32,2560]{1,0:T(8,128)(2,1)S(1)} %add_convert_fusion.2), channel_id=1, source_target_pairs={{0,19},{1,16},{2,17},{3,18},{4,23},{5,20},{6,21},{7,22},{8,27},{9,... | collective-permute-start | bytes 491528 | tf_op jit(solution)/shard_map/ppermute | solution.py:30
  77.3 4.7 %collective-permute-done.5.refs_0_ = bf16[32,2560]{1,0:T(8,128)(2,1)S(1)} collective-permute-done((bf16[32,2560]{1,0:T(8,128)(2,1)S(1)}, bf16[32,2560]{1,0:T(8,128)(2,1)S(1)}, u32[]{:S(2)}, u32[]{:S(2)}) %collective-permute-start.5) | collective-permute-done | bytes 163872 | tf_op jit(solution)/shard_map/ppermute | solution.py:30
  82.2 11.1 %collective-permute-done.15.refs_2_ = bf16[32,2560]{1,0:T(8,128)(2,1)S(1)} collective-permute-done((bf16[32,2560]{1,0:T(8,128)(2,1)S(1)}, bf16[32,2560]{1,0:T(8,128)(2,1)S(1)}, u32[]{:S(2)}, u32[]{:S(2)}) %collective-permute-start.15) | collective-permute-done | bytes 163872 | tf_op jit(solution)/shard_map/ppermute | solution.py:30
  93.3 8.9 %collective-permute-done.21.refs_3_ = bf16[32,2560]{1,0:T(8,128)(2,1)S(1)} collective-permute-done((bf16[32,2560]{1,0:T(8,128)(2,1)S(1)}, bf16[32,2560]{1,0:T(8,128)(2,1)S(1)}, u32[]{:S(2)}, u32[]{:S(2)}) %collective-permute-start.21) | collective-permute-done | bytes 163872 | tf_op jit(solution)/shard_map/ppermute | solution.py:30
  102.2 1.8 %final.1 = (bf16[128,2560]{1,0:T(8,128)(2,1)}, bf16[128,2560]{1,0:T(8,128)(2,1)}) custom-call(s32[2]{0:T(128)S(1)} %pad_add_fusion.where_ref, f32[2,128]{1,0:T(2,128)S(1)} %collective-permute-done.info, bf16[32,2560]{1,0:T(8,128)(2,1)S(1)} %collective-permute-done.5.refs_0_, bf16[32,2560]{1,0:T(8,128)(2,1)S(1)} %collective-permute-done.9.refs_1_, ...), custom_call_target="tpu_custom_call" | custom-call | tf_op jit(solution)/shard_map/final/pallas_call | solution.py:396
  104.0 3.1 %shard_map.97 = bf16[2,256,2560]{2,1,0:T(8,128)(2,1)} custom-call(bf16[64,768]{1,0:T(8,128)(2,1)S(1)} %get-tuple-element.50.refs_0_, bf16[64,768]{1,0:T(8,128)(2,1)S(1)} %get-tuple-element.51.refs_1_, bf16[64,768]{1,0:T(8,128)(2,1)S(1)} %get-tuple-element.52.refs_2_, bf16[64,768]{1,0:T(8,128)(2,1)S(1)} %get-tuple-element.53.refs_3_, ...), custom_call_target="tpu_custom_call" | custom-call | tf_op jit(solution)/shard_map/pallas_call | solution.py:42
  107.1 1.9 %shard_map.98 = bf16[1,256,2560]{2,1,0:T(8,128)(2,1)} custom-call(bf16[64,768]{1,0:T(8,128)(2,1)S(1)} %get-tuple-element.50.refs_0_, bf16[64,768]{1,0:T(8,128)(2,1)S(1)} %get-tuple-element.51.refs_1_, bf16[64,768]{1,0:T(8,128)(2,1)S(1)} %get-tuple-element.52.refs_2_, bf16[64,768]{1,0:T(8,128)(2,1)S(1)} %get-tuple-element.53.refs_3_, ...), custom_call_target="tpu_custom_call" | custom-call | tf_op jit(solution)/shard_map/pallas_call | solution.py:42
  (34 shorter events, 3.5 us)
Async XLA Ops:
  0.6 46.6 %collective-permute-start.2 = (bf16[2,256,2560]{2,1,0:T(8,128)(2,1)}, bf16[2,256,2560]{2,1,0:T(8,128)(2,1)S(1)}, u32[]{:S(2)}, u32[]{:S(2)}) collective-permute-start(bf16[2,256,2560]{2,1,0:T(8,128)(2,1)} %bitcast.15), channel_id=1, source_target_pairs={{0,4},{1,5},{2,6},{3,7},{4,0},{5,1},{6,2},{7,3},{8,12},{9,13},{10,... | collective-permute-start | bytes 7864328 | tf_op jit(solution)/shard_map/ppermute | solution.py:30
  1.2 45.1 %collective-permute-start.3 = (bf16[256,2560]{1,0:T(8,128)(2,1)}, bf16[256,2560]{1,0:T(8,128)(2,1)}, u32[]{:S(2)}, u32[]{:S(2)}) collective-permute-start(bf16[256,2560]{1,0:T(8,128)(2,1)} %bitcast.18), channel_id=1, source_target_pairs={{0,4},{1,5},{2,6},{3,7},{4,0},{5,1},{6,2},{7,3},{8,12},{9,13},{10,... | collective-permute-start | bytes 3932168 | tf_op jit(solution)/shard_map/ppermute | solution.py:30
  4.8 28.7 %collective-permute-start.6 = (bf16[2,32,2560]{2,1,0:T(8,128)(2,1)S(1)}, bf16[2,32,2560]{2,1,0:T(8,128)(2,1)S(1)}, u32[]{:S(2)}, u32[]{:S(2)}) collective-permute-start(bf16[2,32,2560]{2,1,0:T(8,128)(2,1)S(1)} %get-tuple-element.37), channel_id=1, source_target_pairs={{0,1},{1,2},{2,3},{3,0},{4,5},{5,6},{6,7},{7,4},{8,9},{9,10},{10,1... | collective-permute-start | bytes 983048 | tf_op jit(solution)/shard_map/ppermute | solution.py:30
  7.9 20.6 %collective-permute-start.10 = (bf16[2,16,2560]{2,1,0:T(8,128)(2,1)S(1)}, bf16[2,16,2560]{2,1,0:T(8,128)(2,1)S(1)}, u32[]{:S(2)}, u32[]{:S(2)}) collective-permute-start(bf16[2,16,2560]{2,1,0:T(8,128)(2,1)S(1)} %get-tuple-element.40), channel_id=1, source_target_pairs={{0,2},{1,3},{2,0},{3,1},{4,6},{5,7},{6,4},{7,5},{8,10},{9,11},{10,... | collective-permute-start | bytes 491528 | tf_op jit(solution)/shard_map/ppermute | solution.py:30
  10.5 21.5 %collective-permute-start.12 = (bf16[2,16,2560]{2,1,0:T(8,128)(2,1)S(1)}, bf16[2,16,2560]{2,1,0:T(8,128)(2,1)S(1)}, u32[]{:S(2)}, u32[]{:S(2)}) collective-permute-start(bf16[2,16,2560]{2,1,0:T(8,128)(2,1)S(1)} %get-tuple-element.41), channel_id=1, source_target_pairs={{0,2},{1,3},{2,0},{3,1},{4,6},{5,7},{6,4},{7,5},{8,10},{9,11},{10,... | collective-permute-start | bytes 491528 | tf_op jit(solution)/shard_map/ppermute | solution.py:30
  28.5 6.9 %collective-permute-start.16 = (bf16[2,16,2560]{2,1,0:T(8,128)(2,1)S(1)}, bf16[2,16,2560]{2,1,0:T(8,128)(2,1)S(1)}, u32[]{:S(2)}, u32[]{:S(2)}) collective-permute-start(bf16[2,16,2560]{2,1,0:T(8,128)(2,1)S(1)} %get-tuple-element.44), channel_id=1, source_target_pairs={{0,3},{1,0},{2,1},{3,2},{4,7},{5,4},{6,5},{7,6},{8,11},{9,8},{10,9... | collective-permute-start | bytes 491528 | tf_op jit(solution)/shard_map/ppermute | solution.py:30
  32.0 11.0 %collective-permute-start.1 = (bf16[2,32,2560]{2,1,0:T(8,128)(2,1)S(1)}, bf16[2,32,2560]{2,1,0:T(8,128)(2,1)S(1)}, u32[]{:S(2)}, u32[]{:S(2)}) collective-permute-start(bf16[2,32,2560]{2,1,0:T(8,128)(2,1)S(1)} %get-tuple-element.32.refs_0_.refs_4_), channel_id=1, source_target_pairs={{0,8},{1,9},{2,10},{3,11},{4,12},{5,13},{6,14},{7,15},{8,0},{9,1},... | collective-permute-start | bytes 983048 | tf_op jit(solution)/shard_map/ppermute | solution.py:30
  33.5 19.0 %collective-permute-start.7 = (bf16[2,32,2560]{2,1,0:T(8,128)(2,1)S(1)}, bf16[2,32,2560]{2,1,0:T(8,128)(2,1)S(1)}, u32[]{:S(2)}, u32[]{:S(2)}) collective-permute-start(bf16[2,32,2560]{2,1,0:T(8,128)(2,1)S(1)} %collective-permute-done.6.refs_0_.refs_6_), channel_id=1, source_target_pairs={{0,8},{1,9},{2,10},{3,11},{4,12},{5,13},{6,14},{7,15},{8,0},{9,1},... | collective-permute-start | bytes 983048 | tf_op jit(solution)/shard_map/ppermute | solution.py:30
  35.4 6.1 %collective-permute-start.18 = (bf16[2,16,2560]{2,1,0:T(8,128)(2,1)S(1)}, bf16[2,16,2560]{2,1,0:T(8,128)(2,1)S(1)}, u32[]{:S(2)}, u32[]{:S(2)}) collective-permute-start(bf16[2,16,2560]{2,1,0:T(8,128)(2,1)S(1)} %get-tuple-element.45), channel_id=1, source_target_pairs={{0,3},{1,0},{2,1},{3,2},{4,7},{5,4},{6,5},{7,6},{8,11},{9,8},{10,9... | collective-permute-start | bytes 491528 | tf_op jit(solution)/shard_map/ppermute | solution.py:30
  41.5 16.2 %collective-permute-start.11 = (bf16[2,16,2560]{2,1,0:T(8,128)(2,1)S(1)}, bf16[2,16,2560]{2,1,0:T(8,128)(2,1)S(1)}, u32[]{:S(2)}, u32[]{:S(2)}) collective-permute-start(bf16[2,16,2560]{2,1,0:T(8,128)(2,1)S(1)} %collective-permute-done.10.refs_0_.refs_8_), channel_id=1, source_target_pairs={{0,8},{1,9},{2,10},{3,11},{4,12},{5,13},{6,14},{7,15},{8,0},{9,1},... | collective-permute-start | bytes 491528 | tf_op jit(solution)/shard_map/ppermute | solution.py:30
  43.0 17.1 %collective-permute-start.13 = (bf16[2,16,2560]{2,1,0:T(8,128)(2,1)S(1)}, bf16[2,16,2560]{2,1,0:T(8,128)(2,1)S(1)}, u32[]{:S(2)}, u32[]{:S(2)}) collective-permute-start(bf16[2,16,2560]{2,1,0:T(8,128)(2,1)S(1)} %collective-permute-done.12.refs_2_.refs_10_), channel_id=1, source_target_pairs={{0,8},{1,9},{2,10},{3,11},{4,12},{5,13},{6,14},{7,15},{8,0},{9,1},... | collective-permute-start | bytes 491528 | tf_op jit(solution)/shard_map/ppermute | solution.py:30
  46.3 19.1 %collective-permute-start.17 = (bf16[2,16,2560]{2,1,0:T(8,128)(2,1)S(1)}, bf16[2,16,2560]{2,1,0:T(8,128)(2,1)S(1)}, u32[]{:S(2)}, u32[]{:S(2)}) collective-permute-start(bf16[2,16,2560]{2,1,0:T(8,128)(2,1)S(1)} %collective-permute-done.16.refs_0_.refs_12_), channel_id=1, source_target_pairs={{0,8},{1,9},{2,10},{3,11},{4,12},{5,13},{6,14},{7,15},{8,0},{9,1},... | collective-permute-start | bytes 491528 | tf_op jit(solution)/shard_map/ppermute | solution.py:30
  47.3 19.1 %collective-permute-start.19 = (bf16[2,16,2560]{2,1,0:T(8,128)(2,1)S(1)}, bf16[2,16,2560]{2,1,0:T(8,128)(2,1)S(1)}, u32[]{:S(2)}, u32[]{:S(2)}) collective-permute-start(bf16[2,16,2560]{2,1,0:T(8,128)(2,1)S(1)} %collective-permute-done.18.refs_2_.refs_14_), channel_id=1, source_target_pairs={{0,8},{1,9},{2,10},{3,11},{4,12},{5,13},{6,14},{7,15},{8,0},{9,1},... | collective-permute-start | bytes 491528 | tf_op jit(solution)/shard_map/ppermute | solution.py:30
  52.5 19.2 %collective-permute-start.4 = (bf16[32,2560]{1,0:T(8,128)(2,1)S(1)}, bf16[32,2560]{1,0:T(8,128)(2,1)S(1)}, u32[]{:S(2)}, u32[]{:S(2)}) collective-permute-start(bf16[32,2560]{1,0:T(8,128)(2,1)S(1)} %get-tuple-element.36), channel_id=1, source_target_pairs={{0,8},{1,9},{2,10},{3,11},{4,12},{5,13},{6,14},{7,15},{8,0},{9,1},... | collective-permute-start | bytes 491528 | tf_op jit(solution)/shard_map/ppermute | solution.py:30
  57.7 19.0 %collective-permute-start = (f32[2,128]{1,0:T(2,128)S(1)}, f32[2,128]{1,0:T(2,128)S(1)}, u32[]{:S(2)}, u32[]{:S(2)}) collective-permute-start(f32[2,128]{1,0:T(2,128)S(1)} %bitcast.13), channel_id=1, source_target_pairs={{0,16},{1,17},{2,18},{3,19},{4,20},{5,21},{6,22},{7,23},{8,24},{9,... | collective-permute-start | bytes 3080 | tf_op jit(solution)/shard_map/ppermute | solution.py:30
  60.1 11.6 %collective-permute-start.8 = (bf16[32,2560]{1,0:T(8,128)(2,1)S(1)}, bf16[32,2560]{1,0:T(8,128)(2,1)S(1)}, u32[]{:S(2)}, u32[]{:S(2)}) collective-permute-start(bf16[32,2560]{1,0:T(8,128)(2,1)S(1)} %get-tuple-element.39), channel_id=1, source_target_pairs={{0,8},{1,9},{2,10},{3,11},{4,12},{5,13},{6,14},{7,15},{8,0},{9,1},... | collective-permute-start | bytes 491528 | tf_op jit(solution)/shard_map/ppermute | solution.py:30
  65.4 8.8 %collective-permute-start.14 = (bf16[32,2560]{1,0:T(8,128)(2,1)S(1)}, bf16[32,2560]{1,0:T(8,128)(2,1)S(1)}, u32[]{:S(2)}, u32[]{:S(2)}) collective-permute-start(bf16[32,2560]{1,0:T(8,128)(2,1)S(1)} %get-tuple-element.43), channel_id=1, source_target_pairs={{0,8},{1,9},{2,10},{3,11},{4,12},{5,13},{6,14},{7,15},{8,0},{9,1},... | collective-permute-start | bytes 491528 | tf_op jit(solution)/shard_map/ppermute | solution.py:30
  70.5 6.2 %collective-permute-start.20 = (bf16[32,2560]{1,0:T(8,128)(2,1)S(1)}, bf16[32,2560]{1,0:T(8,128)(2,1)S(1)}, u32[]{:S(2)}, u32[]{:S(2)}) collective-permute-start(bf16[32,2560]{1,0:T(8,128)(2,1)S(1)} %get-tuple-element.47), channel_id=1, source_target_pairs={{0,8},{1,9},{2,10},{3,11},{4,12},{5,13},{6,14},{7,15},{8,0},{9,1},... | collective-permute-start | bytes 491528 | tf_op jit(solution)/shard_map/ppermute | solution.py:30
  71.7 32.3 %collective-permute-start.22 = (bf16[64,5888]{1,0:T(8,128)(2,1)S(1)}, bf16[64,5888]{1,0:T(8,128)(2,1)S(1)}, u32[]{:S(2)}, u32[]{:S(2)}) collective-permute-start(bf16[64,5888]{1,0:T(8,128)(2,1)S(1)} %get-tuple-element.54), channel_id=1, source_target_pairs={{0,4},{1,5},{2,6},{3,7},{4,0},{5,1},{6,2},{7,3},{8,12},{9,13},{10,... | collective-permute-start | bytes 2261000 | tf_op jit(solution)/shard_map/ppermute | solution.py:30
  71.7 10.2 %collective-permute-start.5 = (bf16[32,2560]{1,0:T(8,128)(2,1)S(1)}, bf16[32,2560]{1,0:T(8,128)(2,1)S(1)}, u32[]{:S(2)}, u32[]{:S(2)}) collective-permute-start(bf16[32,2560]{1,0:T(8,128)(2,1)S(1)} %add_convert_fusion.3), channel_id=1, source_target_pairs={{0,16},{1,17},{2,18},{3,19},{4,20},{5,21},{6,22},{7,23},{8,24},{9,... | collective-permute-start | bytes 491528 | tf_op jit(solution)/shard_map/ppermute | solution.py:30
  74.2 7.8 %collective-permute-start.9 = (bf16[32,2560]{1,0:T(8,128)(2,1)S(1)}, bf16[32,2560]{1,0:T(8,128)(2,1)S(1)}, u32[]{:S(2)}, u32[]{:S(2)}) collective-permute-start(bf16[32,2560]{1,0:T(8,128)(2,1)S(1)} %add_convert_fusion.2), channel_id=1, source_target_pairs={{0,19},{1,16},{2,17},{3,18},{4,23},{5,20},{6,21},{7,22},{8,27},{9,... | collective-permute-start | bytes 491528 | tf_op jit(solution)/shard_map/ppermute | solution.py:30
  76.7 27.3 %collective-permute-start.23 = (bf16[64,5888]{1,0:T(8,128)(2,1)S(1)}, bf16[64,5888]{1,0:T(8,128)(2,1)S(1)}, u32[]{:S(2)}, u32[]{:S(2)}) collective-permute-start(bf16[64,5888]{1,0:T(8,128)(2,1)S(1)} %get-tuple-element.55), channel_id=1, source_target_pairs={{0,4},{1,5},{2,6},{3,7},{4,0},{5,1},{6,2},{7,3},{8,12},{9,13},{10,... | collective-permute-start | bytes 2261000 | tf_op jit(solution)/shard_map/ppermute | solution.py:30
  76.8 27.2 %collective-permute-start.24 = (bf16[64,5888]{1,0:T(8,128)(2,1)S(1)}, bf16[64,5888]{1,0:T(8,128)(2,1)S(1)}, u32[]{:S(2)}, u32[]{:S(2)}) collective-permute-start(bf16[64,5888]{1,0:T(8,128)(2,1)S(1)} %get-tuple-element.56), channel_id=1, source_target_pairs={{0,4},{1,5},{2,6},{3,7},{4,0},{5,1},{6,2},{7,3},{8,12},{9,13},{10,... | collective-permute-start | bytes 2261000 | tf_op jit(solution)/shard_map/ppermute | solution.py:30
  81.9 22.1 %collective-permute-start.25 = (bf16[64,5888]{1,0:T(8,128)(2,1)S(1)}, bf16[64,5888]{1,0:T(8,128)(2,1)S(1)}, u32[]{:S(2)}, u32[]{:S(2)}) collective-permute-start(bf16[64,5888]{1,0:T(8,128)(2,1)S(1)} %get-tuple-element.57), channel_id=1, source_target_pairs={{0,4},{1,5},{2,6},{3,7},{4,0},{5,1},{6,2},{7,3},{8,12},{9,13},{10,... | collective-permute-start | bytes 2261000 | tf_op jit(solution)/shard_map/ppermute | solution.py:30
  81.9 11.4 %collective-permute-start.15 = (bf16[32,2560]{1,0:T(8,128)(2,1)S(1)}, bf16[32,2560]{1,0:T(8,128)(2,1)S(1)}, u32[]{:S(2)}, u32[]{:S(2)}) collective-permute-start(bf16[32,2560]{1,0:T(8,128)(2,1)S(1)} %add_convert_fusion.1), channel_id=1, source_target_pairs={{0,18},{1,19},{2,16},{3,17},{4,22},{5,23},{6,20},{7,21},{8,26},{9,... | collective-permute-start | bytes 491528 | tf_op jit(solution)/shard_map/ppermute | solution.py:30
  93.3 8.9 %collective-permute-start.21 = (bf16[32,2560]{1,0:T(8,128)(2,1)S(1)}, bf16[32,2560]{1,0:T(8,128)(2,1)S(1)}, u32[]{:S(2)}, u32[]{:S(2)}) collective-permute-start(bf16[32,2560]{1,0:T(8,128)(2,1)S(1)} %add_convert_fusion), channel_id=1, source_target_pairs={{0,17},{1,18},{2,19},{3,16},{4,21},{5,22},{6,23},{7,20},{8,25},{9,... | collective-permute-start | bytes 491528 | tf_op jit(solution)/shard_map/ppermute | solution.py:30

commit v2 on v1

--- a/solution.py
+++ b/solution.py
@@ -59,22 +59,18 @@
     section, column = where_ref[0], where_ref[1]
     packed, info, refs = refs[: len(units)], refs[len(units)], refs[len(units) + 1 :]
     tokens_here, cotangent_here, routes_here, gates_here, sems, small_sems = refs
-    rows_here, width = tokens.shape
+    rows_here = tokens.shape[0]
     capacity = rows_here // window
-    blocks = 4 if width % 512 == 0 else 1
-    step = width // blocks
     small = [
         pltpu.make_async_copy(far, near, small_sems.at[which])
         for which, (far, near) in enumerate(((routes, routes_here), (gates, gates_here)))
     ]
-    for copy in small:
+    large = [
+        pltpu.make_async_copy(far, near, sems.at[which])
+        for which, (far, near) in enumerate(((tokens, tokens_here), (cotangent, cotangent_here)))
+    ]
+    for copy in small + large:
         copy.start()
-    copies = []
-    for which, (far, near) in enumerate(((tokens, tokens_here), (cotangent, cotangent_here))):
-        for b in range(blocks):
-            at = pl.ds(b * step, step)
-            copies.append(pltpu.make_async_copy(far.at[:, at], near.at[:, at], sems.at[which, b]))
-            copies[-1].start()
     for copy in small:
         copy.wait()
     expert_of = jnp.full((1, rows_here), -1, jnp.int32)
@@ -101,16 +97,14 @@
         info[i, 1:2] = scale
     scale_column = column_of(weight)
     for which in range(2):
-        for b in range(blocks):
-            at = slice(b * step, (b + 1) * step)
-            copies[which * blocks + b].wait()
-            if which:
-                block = (cotangent_here[:, at].astype(jnp.float32) * scale_column).astype(jnp.bfloat16)
-            else:
-                block = tokens_here[:, at]
-            slots = dot(select, block).astype(jnp.bfloat16)
-            for out, (k, low, high) in zip(packed, units):
-                out[which, :, at] = slots[k * capacity + low : k * capacity + high]
+        large[which].wait()
+        if which:
+            block = (cotangent_here[...].astype(jnp.float32) * scale_column).astype(jnp.bfloat16)
+        else:
+            block = tokens_here[...]
+        slots = dot(select, block).astype(jnp.bfloat16)
+        for out, (k, low, high) in zip(packed, units):
+            out[which] = slots[k * capacity + low : k * capacity + high]
 
 
 def fetch_body(blocks, gate_up, down, gate_up_out, down_out, sems):
@@ -291,7 +285,6 @@
     f32 = functools.partial(jax.ShapeDtypeStruct, dtype=jnp.float32)
 
     units, chunks = plan(window, capacity)
-    step = width // 4 if width % 512 == 0 else width
     *packed, info = pl.pallas_call(
         functools.partial(pack_body, window, units, lanes),
         out_shape=[bf16((2, high - low, width)) for _, low, high in units] + [f32((len(lanes), 2, rows_here))],
@@ -299,7 +292,7 @@
         out_specs=[IN_VMEM] * (len(units) + 1),
         scratch_shapes=[pltpu.VMEM((rows_here, width), jnp.bfloat16)] * 2
         + [pltpu.VMEM((routes.shape[2], 1, rows_here), dtype) for dtype in (routes.dtype, gates.dtype)]
-        + [pltpu.SemaphoreType.DMA((2, width // step)), pltpu.SemaphoreType.DMA((2,))],
+        + [pltpu.SemaphoreType.DMA((2,)), pltpu.SemaphoreType.DMA((2,))],
         compiler_params=pltpu.CompilerParams(vmem_limit_bytes=12 << 20),
         name="pack",
     )(
@@ -392,7 +385,7 @@
     results = []
     for i, (kind, _) in enumerate(lanes):
         count = len(modes[kind])
-        blocks = width // step
+        blocks = 2
         results += pl.pallas_call(
             functools.partial(final_body, modes[kind], returns, blocks),
             out_shape=[bf16((rows_here, width))] * count,

time: 109 us -> 108 us (level)
  Pallas kernels: 29 us -> 27.9 us
    pallas_call x1, Pallas kernels: 3.49 us -> 2.32 us  [computed(): pl.pallas_call(functools.partial(pack_body, window, units, lanes), out_sh...]
  transfers between devices with their start and end apart: 26 -> 26, of which waited for: 8 -> 8; matrix products, arithmetic and copies ran while one was open for 0% -> 0% of each run, Pallas kernels for 22% -> 21%
where the time goes in v2:
time: 108 us
  waiting for transfers between devices  49.7 us (46%)
  starting transfers between devices  29.3 us (27%)
  Pallas kernels  27.9 us (26%)
    ppermute x26, waiting for transfers between devices, moved(): return lax.ppermute(value, AXES, pairs)  49.7 us
    ppermute x26, starting transfers between devices, moved(): return lax.ppermute(value, AXES, pairs)  29.3 us
    pallas_call x6, Pallas kernels, call(): pl.pallas_call(body, out_shape=outs, in_specs=[IN_SMEM] * smem + [IN_VMEM...  21.6 us
    pallas_call x1, Pallas kernels, computed(): pl.pallas_call(functools.partial(pack_body, window, units, lanes), out_sh...  2.32 us
  transfers between devices with their start and end apart: 26, of which 8 were waited for; matrix products, arithmetic and copies ran while one was open for 0% of the time, Pallas kernels for 21%

profile of v2, /device:TPU:0, one launch (start us, length us, event | category | flops | bytes accessed | tf_op | source)
XLA Modules:
  0.0 108.0 jit_solution(13547961694158787465)
XLA Ops:
  1.3 2.3 %pack.1 = (bf16[2,32,2560]{2,1,0:T(8,128)(2,1)S(1)}, bf16[2,32,2560]{2,1,0:T(8,128)(2,1)S(1)}, bf16[2,16,2560]{2,1,0:T(8,128)(2,1)S(1)}, bf16[2,16,2560]{2,1,0:T...) custom-call(s32[2]{0:T(128)S(1)} %pad_add_fusion.where_ref, ...), custom_call_target="tpu_custom_call" | custom-call | tf_op jit(solution)/shard_map/pack/pallas_call | solution.py:288
  3.7 3.0 %collective-permute-start.6 = (bf16[2,32,2560]{2,1,0:T(8,128)(2,1)S(1)}, bf16[2,32,2560]{2,1,0:T(8,128)(2,1)S(1)}, u32[]{:S(2)}, u32[]{:S(2)}) collective-permute-start(bf16[2,32,2560]{2,1,0:T(8,128)(2,1)S(1)} %get-tuple-element.37), channel_id=1, source_target_pairs={{0,1},{1,2},{2,3},{3,0},{4,5},{5,6},{6,7},{7,4},{8,9},{9,10},{10,1... | collective-permute-start | bytes 983048 | tf_op jit(solution)/shard_map/ppermute | solution.py:30
  6.7 2.6 %collective-permute-start.10 = (bf16[2,16,2560]{2,1,0:T(8,128)(2,1)S(1)}, bf16[2,16,2560]{2,1,0:T(8,128)(2,1)S(1)}, u32[]{:S(2)}, u32[]{:S(2)}) collective-permute-start(bf16[2,16,2560]{2,1,0:T(8,128)(2,1)S(1)} %get-tuple-element.40), channel_id=1, source_target_pairs={{0,2},{1,3},{2,0},{3,1},{4,6},{5,7},{6,4},{7,5},{8,10},{9,11},{10,... | collective-permute-start | bytes 491528 | tf_op jit(solution)/shard_map/ppermute | solution.py:30
  9.6 17.7 %collective-permute-done.10.refs_0_.refs_8_ = bf16[2,16,2560]{2,1,0:T(8,128)(2,1)S(1)} collective-permute-done((bf16[2,16,2560]{2,1,0:T(8,128)(2,1)S(1)}, bf16[2,16,2560]{2,1,0:T(8,128)(2,1)S(1)}, u32[]{:S(2)}, u32[]{:S(2)}) %collective-permute-start.10) | collective-permute-done | bytes 163872 | tf_op jit(solution)/shard_map/ppermute | solution.py:30
  27.3 2.4 %collective-permute-start.16 = (bf16[2,16,2560]{2,1,0:T(8,128)(2,1)S(1)}, bf16[2,16,2560]{2,1,0:T(8,128)(2,1)S(1)}, u32[]{:S(2)}, u32[]{:S(2)}) collective-permute-start(bf16[2,16,2560]{2,1,0:T(8,128)(2,1)S(1)} %get-tuple-element.44), channel_id=1, source_target_pairs={{0,3},{1,0},{2,1},{3,2},{4,7},{5,4},{6,5},{7,6},{8,11},{9,8},{10,9... | collective-permute-start | bytes 491528 | tf_op jit(solution)/shard_map/ppermute | solution.py:30
  29.7 1.1 %collective-permute-done.12.refs_2_.refs_10_ = bf16[2,16,2560]{2,1,0:T(8,128)(2,1)S(1)} collective-permute-done((bf16[2,16,2560]{2,1,0:T(8,128)(2,1)S(1)}, bf16[2,16,2560]{2,1,0:T(8,128)(2,1)S(1)}, u32[]{:S(2)}, u32[]{:S(2)}) %collective-permute-start.12) | collective-permute-done | bytes 163872 | tf_op jit(solution)/shard_map/ppermute | solution.py:30
  30.8 1.5 %collective-permute-start.1 = (bf16[2,32,2560]{2,1,0:T(8,128)(2,1)S(1)}, bf16[2,32,2560]{2,1,0:T(8,128)(2,1)S(1)}, u32[]{:S(2)}, u32[]{:S(2)}) collective-permute-start(bf16[2,32,2560]{2,1,0:T(8,128)(2,1)S(1)} %get-tuple-element.32.refs_0_.refs_4_), channel_id=1, source_target_pairs={{0,8},{1,9},{2,10},{3,11},{4,12},{5,13},{6,14},{7,15},{8,0},{9,1},... | collective-permute-start | bytes 983048 | tf_op jit(solution)/shard_map/ppermute | solution.py:30
  32.9 1.4 %collective-permute-done.16.refs_0_.refs_12_ = bf16[2,16,2560]{2,1,0:T(8,128)(2,1)S(1)} collective-permute-done((bf16[2,16,2560]{2,1,0:T(8,128)(2,1)S(1)}, bf16[2,16,2560]{2,1,0:T(8,128)(2,1)S(1)}, u32[]{:S(2)}, u32[]{:S(2)}) %collective-permute-start.16) | collective-permute-done | bytes 163872 | tf_op jit(solution)/shard_map/ppermute | solution.py:30
  34.3 2.6 %collective-permute-start.18 = (bf16[2,16,2560]{2,1,0:T(8,128)(2,1)S(1)}, bf16[2,16,2560]{2,1,0:T(8,128)(2,1)S(1)}, u32[]{:S(2)}, u32[]{:S(2)}) collective-permute-start(bf16[2,16,2560]{2,1,0:T(8,128)(2,1)S(1)} %get-tuple-element.45), channel_id=1, source_target_pairs={{0,3},{1,0},{2,1},{3,2},{4,7},{5,4},{6,5},{7,6},{8,11},{9,8},{10,9... | collective-permute-start | bytes 491528 | tf_op jit(solution)/shard_map/ppermute | solution.py:30
  36.9 3.5 %collective-permute-done.18.refs_2_.refs_14_ = bf16[2,16,2560]{2,1,0:T(8,128)(2,1)S(1)} collective-permute-done((bf16[2,16,2560]{2,1,0:T(8,128)(2,1)S(1)}, bf16[2,16,2560]{2,1,0:T(8,128)(2,1)S(1)}, u32[]{:S(2)}, u32[]{:S(2)}) %collective-permute-start.18) | collective-permute-done | bytes 163872 | tf_op jit(solution)/shard_map/ppermute | solution.py:30
  40.3 1.5 %collective-permute-start.11 = (bf16[2,16,2560]{2,1,0:T(8,128)(2,1)S(1)}, bf16[2,16,2560]{2,1,0:T(8,128)(2,1)S(1)}, u32[]{:S(2)}, u32[]{:S(2)}) collective-permute-start(bf16[2,16,2560]{2,1,0:T(8,128)(2,1)S(1)} %collective-permute-done.10.refs_0_.refs_8_), channel_id=1, source_target_pairs={{0,8},{1,9},{2,10},{3,11},{4,12},{5,13},{6,14},{7,15},{8,0},{9,1},... | collective-permute-start | bytes 491528 | tf_op jit(solution)/shard_map/ppermute | solution.py:30
  41.9 1.1 %collective-permute-start.13 = (bf16[2,16,2560]{2,1,0:T(8,128)(2,1)S(1)}, bf16[2,16,2560]{2,1,0:T(8,128)(2,1)S(1)}, u32[]{:S(2)}, u32[]{:S(2)}) collective-permute-start(bf16[2,16,2560]{2,1,0:T(8,128)(2,1)S(1)} %collective-permute-done.12.refs_2_.refs_10_), channel_id=1, source_target_pairs={{0,8},{1,9},{2,10},{3,11},{4,12},{5,13},{6,14},{7,15},{8,0},{9,1},... | collective-permute-start | bytes 491528 | tf_op jit(solution)/shard_map/ppermute | solution.py:30
  42.9 2.1 %fetch.1 = (bf16[2,256,2560]{2,1,0:T(8,128)(2,1)S(1)}, bf16[256,2560]{1,0:T(8,128)(2,1)S(1)}) custom-call(bf16[2,256,2560]{2,1,0:T(8,128)(2,1)} %bitcast.16, bf16[256,2560]{1,0:T(8,128)(2,1)} %bitcast.19), custom_call_target="tpu_custom_call" | custom-call | tf_op jit(solution)/shard_map/fetch/pallas_call | solution.py:311
  46.1 1.1 %collective-permute-start.19 = (bf16[2,16,2560]{2,1,0:T(8,128)(2,1)S(1)}, bf16[2,16,2560]{2,1,0:T(8,128)(2,1)S(1)}, u32[]{:S(2)}, u32[]{:S(2)}) collective-permute-start(bf16[2,16,2560]{2,1,0:T(8,128)(2,1)S(1)} %collective-permute-done.18.refs_2_.refs_14_), channel_id=1, source_target_pairs={{0,8},{1,9},{2,10},{3,11},{4,12},{5,13},{6,14},{7,15},{8,0},{9,1},... | collective-permute-start | bytes 491528 | tf_op jit(solution)/shard_map/ppermute | solution.py:30
  47.2 4.1 %shard_map.93 = (f32[32,2560]{1,0:T(8,128)S(1)}, bf16[32,2560]{1,0:T(8,128)(2,1)S(1)}, bf16[64,768]{1,0:T(8,128)(2,1)S(1)}, bf16[64,5888]{1,0:T(8,128)(2,1)S(1)}) custom-call(s32[2]{0:T(128)S(1)} %pad_add_fusion.where_ref, bf16[2,32,2560]{2,1,0:T(8,128)(2,1)S(1)} %get-tuple-element.32.refs_0_.refs_4_, ...), custom_call_target="tpu_custom_call" | custom-call | tf_op jit(solution)/shard_map/pallas_call | solution.py:42
  51.3 1.0 collective-permute-start.4
  52.4 4.1 %shard_map.94 = (f32[32,2560]{1,0:T(8,128)S(1)}, bf16[32,2560]{1,0:T(8,128)(2,1)S(1)}, bf16[64,768]{1,0:T(8,128)(2,1)S(1)}, bf16[64,5888]{1,0:T(8,128)(2,1)S(1)}) custom-call(s32[2]{0:T(128)S(1)} %pad_add_fusion.where_ref, bf16[2,32,2560]{2,1,0:T(8,128)(2,1)S(1)} %collective-permute-done.6.refs_0_.refs_6_, ...), custom_call_target="tpu_custom_call" | custom-call | tf_op jit(solution)/shard_map/pallas_call | solution.py:42
  56.5 2.4 %collective-permute-start = (f32[2,128]{1,0:T(2,128)S(1)}, f32[2,128]{1,0:T(2,128)S(1)}, u32[]{:S(2)}, u32[]{:S(2)}) collective-permute-start(f32[2,128]{1,0:T(2,128)S(1)} %bitcast.13), channel_id=1, source_target_pairs={{0,16},{1,17},{2,18},{3,19},{4,20},{5,21},{6,22},{7,23},{8,24},{9,... | collective-permute-start | bytes 3080 | tf_op jit(solution)/shard_map/ppermute | solution.py:30
  59.0 1.1 %collective-permute-start.8 = (bf16[32,2560]{1,0:T(8,128)(2,1)S(1)}, bf16[32,2560]{1,0:T(8,128)(2,1)S(1)}, u32[]{:S(2)}, u32[]{:S(2)}) collective-permute-start(bf16[32,2560]{1,0:T(8,128)(2,1)S(1)} %get-tuple-element.39), channel_id=1, source_target_pairs={{0,8},{1,9},{2,10},{3,11},{4,12},{5,13},{6,14},{7,15},{8,0},{9,1},... | collective-permute-start | bytes 491528 | tf_op jit(solution)/shard_map/ppermute | solution.py:30
  60.0 4.1 %shard_map.95 = (f32[32,2560]{1,0:T(8,128)S(1)}, bf16[32,2560]{1,0:T(8,128)(2,1)S(1)}, bf16[64,768]{1,0:T(8,128)(2,1)S(1)}, bf16[64,5888]{1,0:T(8,128)(2,1)S(1)}) custom-call(s32[2]{0:T(128)S(1)} %pad_add_fusion.where_ref, bf16[2,16,2560]{2,1,0:T(8,128)(2,1)S(1)} %collective-permute-done.10.refs_0_.refs_8_, ...), custom_call_target="tpu_custom_call" | custom-call | tf_op jit(solution)/shard_map/pallas_call | solution.py:42
  64.2 1.0 collective-permute-start.14
  65.2 4.2 %shard_map.96 = (f32[32,2560]{1,0:T(8,128)S(1)}, bf16[32,2560]{1,0:T(8,128)(2,1)S(1)}, bf16[64,768]{1,0:T(8,128)(2,1)S(1)}, bf16[64,5888]{1,0:T(8,128)(2,1)S(1)}) custom-call(s32[2]{0:T(128)S(1)} %pad_add_fusion.where_ref, bf16[2,16,2560]{2,1,0:T(8,128)(2,1)S(1)} %collective-permute-done.16.refs_0_.refs_12_, ...), custom_call_target="tpu_custom_call" | custom-call | tf_op jit(solution)/shard_map/pallas_call | solution.py:42
  69.4 1.2 %collective-permute-start.20 = (bf16[32,2560]{1,0:T(8,128)(2,1)S(1)}, bf16[32,2560]{1,0:T(8,128)(2,1)S(1)}, u32[]{:S(2)}, u32[]{:S(2)}) collective-permute-start(bf16[32,2560]{1,0:T(8,128)(2,1)S(1)} %get-tuple-element.47), channel_id=1, source_target_pairs={{0,8},{1,9},{2,10},{3,11},{4,12},{5,13},{6,14},{7,15},{8,0},{9,1},... | collective-permute-start | bytes 491528 | tf_op jit(solution)/shard_map/ppermute | solution.py:30
  70.6 1.0 collective-permute-start.5
  71.6 1.4 %collective-permute-done.14 = bf16[32,2560]{1,0:T(8,128)(2,1)S(1)} collective-permute-done((bf16[32,2560]{1,0:T(8,128)(2,1)S(1)}, bf16[32,2560]{1,0:T(8,128)(2,1)S(1)}, u32[]{:S(2)}, u32[]{:S(2)}) %collective-permute-start.14) | collective-permute-done | bytes 163872 | tf_op jit(solution)/shard_map/ppermute | solution.py:30
  73.0 2.5 %collective-permute-start.9 = (bf16[32,2560]{1,0:T(8,128)(2,1)S(1)}, bf16[32,2560]{1,0:T(8,128)(2,1)S(1)}, u32[]{:S(2)}, u32[]{:S(2)}) collective-permute-start(bf16[32,2560]{1,0:T(8,128)(2,1)S(1)} %add_convert_fusion.2), channel_id=1, source_target_pairs={{0,19},{1,16},{2,17},{3,18},{4,23},{5,20},{6,21},{7,22},{8,27},{9,... | collective-permute-start | bytes 491528 | tf_op jit(solution)/shard_map/ppermute | solution.py:30
  76.1 4.7 %collective-permute-done.5.refs_0_ = bf16[32,2560]{1,0:T(8,128)(2,1)S(1)} collective-permute-done((bf16[32,2560]{1,0:T(8,128)(2,1)S(1)}, bf16[32,2560]{1,0:T(8,128)(2,1)S(1)}, u32[]{:S(2)}, u32[]{:S(2)}) %collective-permute-start.5) | collective-permute-done | bytes 163872 | tf_op jit(solution)/shard_map/ppermute | solution.py:30
  81.0 11.2 %collective-permute-done.15.refs_2_ = bf16[32,2560]{1,0:T(8,128)(2,1)S(1)} collective-permute-done((bf16[32,2560]{1,0:T(8,128)(2,1)S(1)}, bf16[32,2560]{1,0:T(8,128)(2,1)S(1)}, u32[]{:S(2)}, u32[]{:S(2)}) %collective-permute-start.15) | collective-permute-done | bytes 163872 | tf_op jit(solution)/shard_map/ppermute | solution.py:30
  92.2 8.9 %collective-permute-done.21.refs_3_ = bf16[32,2560]{1,0:T(8,128)(2,1)S(1)} collective-permute-done((bf16[32,2560]{1,0:T(8,128)(2,1)S(1)}, bf16[32,2560]{1,0:T(8,128)(2,1)S(1)}, u32[]{:S(2)}, u32[]{:S(2)}) %collective-permute-start.21) | collective-permute-done | bytes 163872 | tf_op jit(solution)/shard_map/ppermute | solution.py:30
  101.0 1.9 %final.1 = (bf16[128,2560]{1,0:T(8,128)(2,1)}, bf16[128,2560]{1,0:T(8,128)(2,1)}) custom-call(s32[2]{0:T(128)S(1)} %pad_add_fusion.where_ref, f32[2,128]{1,0:T(2,128)S(1)} %collective-permute-done.info, bf16[32,2560]{1,0:T(8,128)(2,1)S(1)} %collective-permute-done.5.refs_0_, bf16[32,2560]{1,0:T(8,128)(2,1)S(1)} %collective-permute-done.9.refs_1_, ...), custom_call_target="tpu_custom_call" | custom-call | tf_op jit(solution)/shard_map/final/pallas_call | solution.py:389
  103.0 3.1 %shard_map.97 = bf16[2,256,2560]{2,1,0:T(8,128)(2,1)} custom-call(bf16[64,768]{1,0:T(8,128)(2,1)S(1)} %get-tuple-element.50.refs_0_, bf16[64,768]{1,0:T(8,128)(2,1)S(1)} %get-tuple-element.51.refs_1_, bf16[64,768]{1,0:T(8,128)(2,1)S(1)} %get-tuple-element.52.refs_2_, bf16[64,768]{1,0:T(8,128)(2,1)S(1)} %get-tuple-element.53.refs_3_, ...), custom_call_target="tpu_custom_call" | custom-call | tf_op jit(solution)/shard_map/pallas_call | solution.py:42
  106.1 1.9 %shard_map.98 = bf16[1,256,2560]{2,1,0:T(8,128)(2,1)} custom-call(bf16[64,768]{1,0:T(8,128)(2,1)S(1)} %get-tuple-element.50.refs_0_, bf16[64,768]{1,0:T(8,128)(2,1)S(1)} %get-tuple-element.51.refs_1_, bf16[64,768]{1,0:T(8,128)(2,1)S(1)} %get-tuple-element.52.refs_2_, bf16[64,768]{1,0:T(8,128)(2,1)S(1)} %get-tuple-element.53.refs_3_, ...), custom_call_target="tpu_custom_call" | custom-call | tf_op jit(solution)/shard_map/pallas_call | solution.py:42
  (34 shorter events, 3.5 us)
Async XLA Ops:
  0.6 45.5 %collective-permute-start.2 = (bf16[2,256,2560]{2,1,0:T(8,128)(2,1)}, bf16[2,256,2560]{2,1,0:T(8,128)(2,1)S(1)}, u32[]{:S(2)}, u32[]{:S(2)}) collective-permute-start(bf16[2,256,2560]{2,1,0:T(8,128)(2,1)} %bitcast.15), channel_id=1, source_target_pairs={{0,4},{1,5},{2,6},{3,7},{4,0},{5,1},{6,2},{7,3},{8,12},{9,13},{10,... | collective-permute-start | bytes 7864328 | tf_op jit(solution)/shard_map/ppermute | solution.py:30
  1.2 43.9 %collective-permute-start.3 = (bf16[256,2560]{1,0:T(8,128)(2,1)}, bf16[256,2560]{1,0:T(8,128)(2,1)}, u32[]{:S(2)}, u32[]{:S(2)}) collective-permute-start(bf16[256,2560]{1,0:T(8,128)(2,1)} %bitcast.18), channel_id=1, source_target_pairs={{0,4},{1,5},{2,6},{3,7},{4,0},{5,1},{6,2},{7,3},{8,12},{9,13},{10,... | collective-permute-start | bytes 3932168 | tf_op jit(solution)/shard_map/ppermute | solution.py:30
  3.7 28.7 %collective-permute-start.6 = (bf16[2,32,2560]{2,1,0:T(8,128)(2,1)S(1)}, bf16[2,32,2560]{2,1,0:T(8,128)(2,1)S(1)}, u32[]{:S(2)}, u32[]{:S(2)}) collective-permute-start(bf16[2,32,2560]{2,1,0:T(8,128)(2,1)S(1)} %get-tuple-element.37), channel_id=1, source_target_pairs={{0,1},{1,2},{2,3},{3,0},{4,5},{5,6},{6,7},{7,4},{8,9},{9,10},{10,1... | collective-permute-start | bytes 983048 | tf_op jit(solution)/shard_map/ppermute | solution.py:30
  6.7 20.6 %collective-permute-start.10 = (bf16[2,16,2560]{2,1,0:T(8,128)(2,1)S(1)}, bf16[2,16,2560]{2,1,0:T(8,128)(2,1)S(1)}, u32[]{:S(2)}, u32[]{:S(2)}) collective-permute-start(bf16[2,16,2560]{2,1,0:T(8,128)(2,1)S(1)} %get-tuple-element.40), channel_id=1, source_target_pairs={{0,2},{1,3},{2,0},{3,1},{4,6},{5,7},{6,4},{7,5},{8,10},{9,11},{10,... | collective-permute-start | bytes 491528 | tf_op jit(solution)/shard_map/ppermute | solution.py:30
  9.3 21.5 %collective-permute-start.12 = (bf16[2,16,2560]{2,1,0:T(8,128)(2,1)S(1)}, bf16[2,16,2560]{2,1,0:T(8,128)(2,1)S(1)}, u32[]{:S(2)}, u32[]{:S(2)}) collective-permute-start(bf16[2,16,2560]{2,1,0:T(8,128)(2,1)S(1)} %get-tuple-element.41), channel_id=1, source_target_pairs={{0,2},{1,3},{2,0},{3,1},{4,6},{5,7},{6,4},{7,5},{8,10},{9,11},{10,... | collective-permute-start | bytes 491528 | tf_op jit(solution)/shard_map/ppermute | solution.py:30
  27.3 6.9 %collective-permute-start.16 = (bf16[2,16,2560]{2,1,0:T(8,128)(2,1)S(1)}, bf16[2,16,2560]{2,1,0:T(8,128)(2,1)S(1)}, u32[]{:S(2)}, u32[]{:S(2)}) collective-permute-start(bf16[2,16,2560]{2,1,0:T(8,128)(2,1)S(1)} %get-tuple-element.44), channel_id=1, source_target_pairs={{0,3},{1,0},{2,1},{3,2},{4,7},{5,4},{6,5},{7,6},{8,11},{9,8},{10,9... | collective-permute-start | bytes 491528 | tf_op jit(solution)/shard_map/ppermute | solution.py:30
  30.8 11.0 %collective-permute-start.1 = (bf16[2,32,2560]{2,1,0:T(8,128)(2,1)S(1)}, bf16[2,32,2560]{2,1,0:T(8,128)(2,1)S(1)}, u32[]{:S(2)}, u32[]{:S(2)}) collective-permute-start(bf16[2,32,2560]{2,1,0:T(8,128)(2,1)S(1)} %get-tuple-element.32.refs_0_.refs_4_), channel_id=1, source_target_pairs={{0,8},{1,9},{2,10},{3,11},{4,12},{5,13},{6,14},{7,15},{8,0},{9,1},... | collective-permute-start | bytes 983048 | tf_op jit(solution)/shard_map/ppermute | solution.py:30
  32.4 19.0 %collective-permute-start.7 = (bf16[2,32,2560]{2,1,0:T(8,128)(2,1)S(1)}, bf16[2,32,2560]{2,1,0:T(8,128)(2,1)S(1)}, u32[]{:S(2)}, u32[]{:S(2)}) collective-permute-start(bf16[2,32,2560]{2,1,0:T(8,128)(2,1)S(1)} %collective-permute-done.6.refs_0_.refs_6_), channel_id=1, source_target_pairs={{0,8},{1,9},{2,10},{3,11},{4,12},{5,13},{6,14},{7,15},{8,0},{9,1},... | collective-permute-start | bytes 983048 | tf_op jit(solution)/shard_map/ppermute | solution.py:30
  34.3 6.1 %collective-permute-start.18 = (bf16[2,16,2560]{2,1,0:T(8,128)(2,1)S(1)}, bf16[2,16,2560]{2,1,0:T(8,128)(2,1)S(1)}, u32[]{:S(2)}, u32[]{:S(2)}) collective-permute-start(bf16[2,16,2560]{2,1,0:T(8,128)(2,1)S(1)} %get-tuple-element.45), channel_id=1, source_target_pairs={{0,3},{1,0},{2,1},{3,2},{4,7},{5,4},{6,5},{7,6},{8,11},{9,8},{10,9... | collective-permute-start | bytes 491528 | tf_op jit(solution)/shard_map/ppermute | solution.py:30
  40.3 16.2 %collective-permute-start.11 = (bf16[2,16,2560]{2,1,0:T(8,128)(2,1)S(1)}, bf16[2,16,2560]{2,1,0:T(8,128)(2,1)S(1)}, u32[]{:S(2)}, u32[]{:S(2)}) collective-permute-start(bf16[2,16,2560]{2,1,0:T(8,128)(2,1)S(1)} %collective-permute-done.10.refs_0_.refs_8_), channel_id=1, source_target_pairs={{0,8},{1,9},{2,10},{3,11},{4,12},{5,13},{6,14},{7,15},{8,0},{9,1},... | collective-permute-start | bytes 491528 | tf_op jit(solution)/shard_map/ppermute | solution.py:30
  41.9 17.1 %collective-permute-start.13 = (bf16[2,16,2560]{2,1,0:T(8,128)(2,1)S(1)}, bf16[2,16,2560]{2,1,0:T(8,128)(2,1)S(1)}, u32[]{:S(2)}, u32[]{:S(2)}) collective-permute-start(bf16[2,16,2560]{2,1,0:T(8,128)(2,1)S(1)} %collective-permute-done.12.refs_2_.refs_10_), channel_id=1, source_target_pairs={{0,8},{1,9},{2,10},{3,11},{4,12},{5,13},{6,14},{7,15},{8,0},{9,1},... | collective-permute-start | bytes 491528 | tf_op jit(solution)/shard_map/ppermute | solution.py:30
  45.1 19.1 %collective-permute-start.17 = (bf16[2,16,2560]{2,1,0:T(8,128)(2,1)S(1)}, bf16[2,16,2560]{2,1,0:T(8,128)(2,1)S(1)}, u32[]{:S(2)}, u32[]{:S(2)}) collective-permute-start(bf16[2,16,2560]{2,1,0:T(8,128)(2,1)S(1)} %collective-permute-done.16.refs_0_.refs_12_), channel_id=1, source_target_pairs={{0,8},{1,9},{2,10},{3,11},{4,12},{5,13},{6,14},{7,15},{8,0},{9,1},... | collective-permute-start | bytes 491528 | tf_op jit(solution)/shard_map/ppermute | solution.py:30
  46.1 19.1 %collective-permute-start.19 = (bf16[2,16,2560]{2,1,0:T(8,128)(2,1)S(1)}, bf16[2,16,2560]{2,1,0:T(8,128)(2,1)S(1)}, u32[]{:S(2)}, u32[]{:S(2)}) collective-permute-start(bf16[2,16,2560]{2,1,0:T(8,128)(2,1)S(1)} %collective-permute-done.18.refs_2_.refs_14_), channel_id=1, source_target_pairs={{0,8},{1,9},{2,10},{3,11},{4,12},{5,13},{6,14},{7,15},{8,0},{9,1},... | collective-permute-start | bytes 491528 | tf_op jit(solution)/shard_map/ppermute | solution.py:30
  51.3 19.2 %collective-permute-start.4 = (bf16[32,2560]{1,0:T(8,128)(2,1)S(1)}, bf16[32,2560]{1,0:T(8,128)(2,1)S(1)}, u32[]{:S(2)}, u32[]{:S(2)}) collective-permute-start(bf16[32,2560]{1,0:T(8,128)(2,1)S(1)} %get-tuple-element.36), channel_id=1, source_target_pairs={{0,8},{1,9},{2,10},{3,11},{4,12},{5,13},{6,14},{7,15},{8,0},{9,1},... | collective-permute-start | bytes 491528 | tf_op jit(solution)/shard_map/ppermute | solution.py:30
  56.5 19.0 %collective-permute-start = (f32[2,128]{1,0:T(2,128)S(1)}, f32[2,128]{1,0:T(2,128)S(1)}, u32[]{:S(2)}, u32[]{:S(2)}) collective-permute-start(f32[2,128]{1,0:T(2,128)S(1)} %bitcast.13), channel_id=1, source_target_pairs={{0,16},{1,17},{2,18},{3,19},{4,20},{5,21},{6,22},{7,23},{8,24},{9,... | collective-permute-start | bytes 3080 | tf_op jit(solution)/shard_map/ppermute | solution.py:30
  59.0 11.6 %collective-permute-start.8 = (bf16[32,2560]{1,0:T(8,128)(2,1)S(1)}, bf16[32,2560]{1,0:T(8,128)(2,1)S(1)}, u32[]{:S(2)}, u32[]{:S(2)}) collective-permute-start(bf16[32,2560]{1,0:T(8,128)(2,1)S(1)} %get-tuple-element.39), channel_id=1, source_target_pairs={{0,8},{1,9},{2,10},{3,11},{4,12},{5,13},{6,14},{7,15},{8,0},{9,1},... | collective-permute-start | bytes 491528 | tf_op jit(solution)/shard_map/ppermute | solution.py:30
  64.2 8.8 %collective-permute-start.14 = (bf16[32,2560]{1,0:T(8,128)(2,1)S(1)}, bf16[32,2560]{1,0:T(8,128)(2,1)S(1)}, u32[]{:S(2)}, u32[]{:S(2)}) collective-permute-start(bf16[32,2560]{1,0:T(8,128)(2,1)S(1)} %get-tuple-element.43), channel_id=1, source_target_pairs={{0,8},{1,9},{2,10},{3,11},{4,12},{5,13},{6,14},{7,15},{8,0},{9,1},... | collective-permute-start | bytes 491528 | tf_op jit(solution)/shard_map/ppermute | solution.py:30
  69.4 6.2 %collective-permute-start.20 = (bf16[32,2560]{1,0:T(8,128)(2,1)S(1)}, bf16[32,2560]{1,0:T(8,128)(2,1)S(1)}, u32[]{:S(2)}, u32[]{:S(2)}) collective-permute-start(bf16[32,2560]{1,0:T(8,128)(2,1)S(1)} %get-tuple-element.47), channel_id=1, source_target_pairs={{0,8},{1,9},{2,10},{3,11},{4,12},{5,13},{6,14},{7,15},{8,0},{9,1},... | collective-permute-start | bytes 491528 | tf_op jit(solution)/shard_map/ppermute | solution.py:30
  70.5 32.4 %collective-permute-start.22 = (bf16[64,5888]{1,0:T(8,128)(2,1)S(1)}, bf16[64,5888]{1,0:T(8,128)(2,1)S(1)}, u32[]{:S(2)}, u32[]{:S(2)}) collective-permute-start(bf16[64,5888]{1,0:T(8,128)(2,1)S(1)} %get-tuple-element.54), channel_id=1, source_target_pairs={{0,4},{1,5},{2,6},{3,7},{4,0},{5,1},{6,2},{7,3},{8,12},{9,13},{10,... | collective-permute-start | bytes 2261000 | tf_op jit(solution)/shard_map/ppermute | solution.py:30
  70.6 10.2 %collective-permute-start.5 = (bf16[32,2560]{1,0:T(8,128)(2,1)S(1)}, bf16[32,2560]{1,0:T(8,128)(2,1)S(1)}, u32[]{:S(2)}, u32[]{:S(2)}) collective-permute-start(bf16[32,2560]{1,0:T(8,128)(2,1)S(1)} %add_convert_fusion.3), channel_id=1, source_target_pairs={{0,16},{1,17},{2,18},{3,19},{4,20},{5,21},{6,22},{7,23},{8,24},{9,... | collective-permute-start | bytes 491528 | tf_op jit(solution)/shard_map/ppermute | solution.py:30
  73.0 7.7 %collective-permute-start.9 = (bf16[32,2560]{1,0:T(8,128)(2,1)S(1)}, bf16[32,2560]{1,0:T(8,128)(2,1)S(1)}, u32[]{:S(2)}, u32[]{:S(2)}) collective-permute-start(bf16[32,2560]{1,0:T(8,128)(2,1)S(1)} %add_convert_fusion.2), channel_id=1, source_target_pairs={{0,19},{1,16},{2,17},{3,18},{4,23},{5,20},{6,21},{7,22},{8,27},{9,... | collective-permute-start | bytes 491528 | tf_op jit(solution)/shard_map/ppermute | solution.py:30
  75.5 27.4 %collective-permute-start.23 = (bf16[64,5888]{1,0:T(8,128)(2,1)S(1)}, bf16[64,5888]{1,0:T(8,128)(2,1)S(1)}, u32[]{:S(2)}, u32[]{:S(2)}) collective-permute-start(bf16[64,5888]{1,0:T(8,128)(2,1)S(1)} %get-tuple-element.55), channel_id=1, source_target_pairs={{0,4},{1,5},{2,6},{3,7},{4,0},{5,1},{6,2},{7,3},{8,12},{9,13},{10,... | collective-permute-start | bytes 2261000 | tf_op jit(solution)/shard_map/ppermute | solution.py:30
  75.6 27.4 %collective-permute-start.24 = (bf16[64,5888]{1,0:T(8,128)(2,1)S(1)}, bf16[64,5888]{1,0:T(8,128)(2,1)S(1)}, u32[]{:S(2)}, u32[]{:S(2)}) collective-permute-start(bf16[64,5888]{1,0:T(8,128)(2,1)S(1)} %get-tuple-element.56), channel_id=1, source_target_pairs={{0,4},{1,5},{2,6},{3,7},{4,0},{5,1},{6,2},{7,3},{8,12},{9,13},{10,... | collective-permute-start | bytes 2261000 | tf_op jit(solution)/shard_map/ppermute | solution.py:30
  80.8 22.2 %collective-permute-start.25 = (bf16[64,5888]{1,0:T(8,128)(2,1)S(1)}, bf16[64,5888]{1,0:T(8,128)(2,1)S(1)}, u32[]{:S(2)}, u32[]{:S(2)}) collective-permute-start(bf16[64,5888]{1,0:T(8,128)(2,1)S(1)} %get-tuple-element.57), channel_id=1, source_target_pairs={{0,4},{1,5},{2,6},{3,7},{4,0},{5,1},{6,2},{7,3},{8,12},{9,13},{10,... | collective-permute-start | bytes 2261000 | tf_op jit(solution)/shard_map/ppermute | solution.py:30
  80.8 11.4 %collective-permute-start.15 = (bf16[32,2560]{1,0:T(8,128)(2,1)S(1)}, bf16[32,2560]{1,0:T(8,128)(2,1)S(1)}, u32[]{:S(2)}, u32[]{:S(2)}) collective-permute-start(bf16[32,2560]{1,0:T(8,128)(2,1)S(1)} %add_convert_fusion.1), channel_id=1, source_target_pairs={{0,18},{1,19},{2,16},{3,17},{4,22},{5,23},{6,20},{7,21},{8,26},{9,... | collective-permute-start | bytes 491528 | tf_op jit(solution)/shard_map/ppermute | solution.py:30
  92.2 8.9 %collective-permute-start.21 = (bf16[32,2560]{1,0:T(8,128)(2,1)S(1)}, bf16[32,2560]{1,0:T(8,128)(2,1)S(1)}, u32[]{:S(2)}, u32[]{:S(2)}) collective-permute-start(bf16[32,2560]{1,0:T(8,128)(2,1)S(1)} %add_convert_fusion), channel_id=1, source_target_pairs={{0,17},{1,18},{2,19},{3,16},{4,21},{5,22},{6,23},{7,20},{8,25},{9,... | collective-permute-start | bytes 491528 | tf_op jit(solution)/shard_map/ppermute | solution.py:30
